TPU v7x, 32 devices: a whole 2x2x4 slice. The times are simulated.
32 devices in a mesh: rows: 8 (over y, x, core), cols: 4 (over z).
Axes of the slice: x: 2, y: 2, z: 4, core: 2. Of those that a mesh axis runs over, the one named last changes fastest.
Arguments:
- terminal_value: float32 [1024, 2048], P('rows', 'cols'), may hold values from -6 to 6
- density_start: float32 [1024, 2048], P('rows', 'cols'), may hold values from 0.2 to 3
- start_cells: int32 [131072], P(('rows', 'cols')), may hold values from 0 to 65535
- offsets: float32 [2, 131072], P(None, ('rows', 'cols')), may hold values from -4 to 4
- weights: float32 [131072], P(('rows', 'cols')), may hold values from 0.3 to 9
- dest_tiles: int32 [1024], P(('rows', 'cols')), may hold values from 0 to 31, as said below
- end_cells: int32 [131072], P(('rows', 'cols')), may hold values from 0 to 65535
Outputs:
- value: float32 [1024, 2048], P('rows', 'cols')
- density: float32 [1024, 2048], P('rows', 'cols')
Inputs may be any that keep to these rules, and one draw needn't show every extreme that they name: `dest_tiles`: block b's tile lies in the band of the tile where b starts or in a band next to it. At most 8 blocks that start in one tile go to any one tile, and for every starting tile there is one destination tile that receives exactly 8 of its blocks.
All inputs are finite; a program needn't handle non-finite values.
Results may differ from a plain program's by a relative error of at most 0.0003.
Values sent between devices are 32-bit elements; how exact they have to be, the bound alone decides.
No kernel may reach another device: no remote copies, remote signals or barrier semaphores. Data moves between devices by JAX's collectives and lax.ppermute only.
A program may use at most 64 MiB of HBM per device.

v0:
```python
import jax
import jax.numpy as jnp
from jax import lax
from jax.sharding import PartitionSpec as P

HJB_STEPS = 4
ITERS = 2


def padded_2(value, sides, width):
    for axis, dim in sides:
        peers, length = (lax.axis_size(axis), value.shape[dim])
        up = [(i, (i + 1) % peers) for i in range(peers - 1)]
        down = [(j, i) for i, j in up]
        last = lax.slice_in_dim(value, length - width, length, axis=dim)
        initial = lax.slice_in_dim(value, 0, width, axis=dim)
        before = lax.ppermute(last, axis, up)
        after = lax.ppermute(initial, axis, down)
        value = jnp.concatenate([before, value, after], axis=dim)
    return value


def from_behind(value, axis, steps):
    count = lax.axis_size(axis)
    initial, last = (max(0, -steps), min(count, count - steps))
    return lax.ppermute(value, axis, [(source, source + steps) for source in range(initial, last)])


def hjb_update(padded, density):
    value = padded[1:-1, 1:-1]
    up = padded[:-2, 1:-1]
    down = padded[2:, 1:-1]
    left = padded[1:-1, :-2]
    right = padded[1:-1, 2:]
    back_x = jnp.maximum(value - up, 0.0)
    fore_x = jnp.minimum(down - value, 0.0)
    back_y = jnp.maximum(value - left, 0.0)
    fore_y = jnp.minimum(right - value, 0.0)
    square_x = jnp.maximum(back_x * back_x, fore_x * fore_x)
    square_y = jnp.maximum(back_y * back_y, fore_y * fore_y)
    spread = up + down + left + right - 4.0 * value
    return value + 0.25 * (0.5 * spread - 0.5 * (square_x + square_y) + 0.5 * density)


def sweep_once(deep_value, density, inside):
    widened = padded_2(density, (("rows", 0), ("cols", 1)), HJB_STEPS)
    current = deep_value
    for inner in range(HJB_STEPS):
        local_density = widened[inner : widened.shape[0] - inner, inner : widened.shape[1] - inner]
        trim = inner + 1
        kept = inside[trim : inside.shape[0] - trim, trim : inside.shape[1] - trim]
        updated = hjb_update(current, local_density)
        current = jnp.where(kept, updated, 0.0)
    return current


def group_size(count, unit, most):
    group = unit
    while count % (group * 2) == 0 and group * 2 <= most:
        group = group * 2
    return group


def route_cells(buffer, n_cols, cap):
    sectioned = buffer.reshape((3, n_cols * cap) + buffer.shape[1:])
    sectioned = lax.all_to_all(sectioned, "cols", split_axis=1, concat_axis=1, tiled=True)
    pieces = [sectioned[1]]
    for section, step in ((0, -1), (2, 1)):
        pieces.append(from_behind(sectioned[section], "rows", step))
    return jnp.concatenate(pieces, axis=0)


def route_moves(buffer, n_cols, cap):
    sectioned = buffer.reshape((3, n_cols * cap) + buffer.shape[1:])
    sectioned = lax.all_to_all(sectioned, "cols", split_axis=1, concat_axis=1, tiled=True)
    pieces = [sectioned[1]]
    for section, step in ((0, -1), (2, 1)):
        pieces.append(from_behind(sectioned[section], "rows", step))
    return jnp.concatenate(pieces, axis=0)


def sample_corners(padded, start_cells, cols_here, block_len):
    rows_pad, cols_pad = padded.shape
    count = start_cells.shape[0]
    group = group_size(count, block_len, 512)
    row_top = (start_cells // cols_here + 1).reshape(-1, group)
    col_left = (start_cells % cols_here + 1).reshape(-1, group)
    row_iota = jnp.arange(rows_pad, dtype=jnp.int32)
    col_iota = jnp.arange(cols_pad, dtype=jnp.int32)

    def step(carry, item):
        top, left = item
        upper_pick = (top[:, None] == row_iota[None, :]).astype(jnp.float32)
        lower_pick = (top[:, None] + 1 == row_iota[None, :]).astype(jnp.float32)
        picks = jnp.concatenate([upper_pick, lower_pick], axis=0)
        lines = jnp.dot(
            picks, padded, precision=lax.Precision.HIGHEST, preferred_element_type=jnp.float32
        )
        upper = lines[:group]
        lower = lines[group:]
        left_mask = left[:, None] == col_iota[None, :]
        right_mask = left[:, None] + 1 == col_iota[None, :]
        corner_a = jnp.sum(jnp.where(left_mask, upper, 0.0), axis=1)
        corner_b = jnp.sum(jnp.where(left_mask, lower, 0.0), axis=1)
        corner_c = jnp.sum(jnp.where(right_mask, upper, 0.0), axis=1)
        corner_d = jnp.sum(jnp.where(right_mask, lower, 0.0), axis=1)
        return (carry, jnp.stack([corner_a, corner_b, corner_c, corner_d], axis=0))

    unused, corners = lax.scan(step, jnp.zeros((), jnp.float32), (row_top, col_left))
    corners = jnp.transpose(corners, (1, 0, 2)).reshape(4, count)
    return (corners[0], corners[1], corners[2], corners[3])


def deposit_mass(arrived, arrived_cells, rows_here, cols_here, n_rows, n_cols):
    block_len = arrived.shape[2]
    move_x = arrived[:, 0].reshape(-1)
    move_y = arrived[:, 1].reshape(-1)
    masses = arrived[:, 2].reshape(-1)
    cells = arrived_cells.reshape(-1)
    count = cells.shape[0]
    group = group_size(count, block_len, 512)
    row_iota = jnp.arange(rows_here + 1, dtype=jnp.int32)
    col_iota = jnp.arange(cols_here + 1, dtype=jnp.int32)

    def step(total, item):
        part_x, part_y, part_mass, part_cells = item
        row_cell = part_cells // cols_here
        col_cell = part_cells % cols_here
        row_side = jnp.where(
            row_iota[None, :] == row_cell[:, None],
            part_mass[:, None] * (1.0 - part_x[:, None]),
            0.0,
        )
        row_side = row_side + jnp.where(
            row_iota[None, :] == row_cell[:, None] + 1, part_mass[:, None] * part_x[:, None], 0.0
        )
        col_side = jnp.where(col_iota[None, :] == col_cell[:, None], 1.0 - part_y[:, None], 0.0)
        col_side = col_side + jnp.where(
            col_iota[None, :] == col_cell[:, None] + 1, part_y[:, None], 0.0
        )
        added = lax.dot_general(
            row_side,
            col_side,
            (((0,), (0,)), ((), ())),
            precision=lax.Precision.HIGHEST,
            preferred_element_type=jnp.float32,
        )
        return (total + added, None)

    items = (
        move_x.reshape(-1, group),
        move_y.reshape(-1, group),
        masses.reshape(-1, group),
        cells.reshape(-1, group),
    )
    grid, unused = lax.scan(step, jnp.zeros((rows_here + 1, cols_here + 1), jnp.float32), items)
    last_band = lax.axis_index("rows") == n_rows - 1
    last_column = lax.axis_index("cols") == n_cols - 1
    spill_row = grid[rows_here]
    below = from_behind(spill_row, "rows", 1)
    upper = grid[:rows_here].at[0].add(below)
    upper = upper.at[rows_here - 1].add(jnp.where(last_band, spill_row, 0.0))
    spill_col = upper[:, cols_here]
    beside = from_behind(spill_col, "cols", 1)
    placed = upper[:, :cols_here].at[:, 0].add(beside)
    return placed.at[:, cols_here - 1].add(jnp.where(last_column, spill_col, 0.0))


def body(terminal_value, density_start, start_cells, offsets, weights, dest_tiles, end_cells):
    rows_here, cols_here = terminal_value.shape
    n_rows = lax.axis_size("rows")
    n_cols = lax.axis_size("cols")
    blocks = dest_tiles.shape[0]
    block_len = weights.shape[0] // blocks
    cap = blocks // 4
    frac_x = 0.5 + 0.45 * jnp.tanh(offsets[0])
    frac_y = 0.5 + 0.45 * jnp.tanh(offsets[1])
    same = dest_tiles[:, None] == dest_tiles[None, :]
    counter = jnp.arange(blocks, dtype=jnp.int32)
    earlier = counter[:, None] > counter[None, :]
    rank = jnp.sum(same & earlier, axis=1)
    my_band = lax.axis_index("rows")
    slots = ((dest_tiles // n_cols - my_band + 1) * n_cols + dest_tiles % n_cols) * cap + rank
    slot_count = 3 * n_cols * cap
    slot_iota = jnp.arange(slot_count, dtype=jnp.int32)
    placing = slot_iota[:, None] == slots[None, :]
    placing_float = placing.astype(jnp.float32)
    cell_blocks = end_cells.reshape(blocks, block_len)
    cell_buffer = jnp.sum(jnp.where(placing[:, :, None], cell_blocks[None, :, :], 0), axis=1)
    arrived_cells = route_cells(cell_buffer, n_cols, cap)
    total_cells = rows_here * cols_here * n_rows * n_cols
    total = lax.psum(jnp.sum(weights), ("rows", "cols"))
    scale = total_cells / total
    depth = HJB_STEPS + 1
    deep_value = padded_2(terminal_value, (("rows", 0), ("cols", 1)), depth)
    global_rows = (
        lax.axis_index("rows") * rows_here
        - depth
        + jnp.arange(rows_here + 2 * depth, dtype=jnp.int32)
    )
    global_cols = (
        lax.axis_index("cols") * cols_here
        - depth
        + jnp.arange(cols_here + 2 * depth, dtype=jnp.int32)
    )
    inside_rows = (global_rows >= 0) & (global_rows < rows_here * n_rows)
    inside_cols = (global_cols >= 0) & (global_cols < cols_here * n_cols)
    inside = inside_rows[:, None] & inside_cols[None, :]
    density = density_start
    value = terminal_value
    for outer in range(ITERS):
        padded = sweep_once(deep_value, density, inside)
        value = padded[1:-1, 1:-1]
        corner_a, corner_b, corner_c, corner_d = sample_corners(
            padded, start_cells, cols_here, block_len
        )
        grad_x = (1.0 - frac_y) * (corner_b - corner_a) + frac_y * (corner_d - corner_c)
        grad_y = (1.0 - frac_x) * (corner_c - corner_a) + frac_x * (corner_d - corner_b)
        moved_x = 0.5 + 0.45 * jnp.tanh(offsets[0] - grad_x)
        moved_y = 0.5 + 0.45 * jnp.tanh(offsets[1] - grad_y)
        payload = jnp.stack(
            [
                moved_x.reshape(blocks, block_len),
                moved_y.reshape(blocks, block_len),
                weights.reshape(blocks, block_len),
            ],
            axis=1,
        )
        move_buffer = jnp.einsum(
            "sb,bkl->skl", placing_float, payload, precision=lax.Precision.HIGHEST
        )
        arrived = route_moves(move_buffer, n_cols, cap)
        deposit = deposit_mass(arrived, arrived_cells, rows_here, cols_here, n_rows, n_cols)
        fresh = deposit * scale
        density = 0.5 * density + 0.5 * fresh
    return (value, density)


def solution(mesh):
    in_specs = (
        P("rows", "cols"),
        P("rows", "cols"),
        P(("rows", "cols")),
        P(None, ("rows", "cols")),
        P(("rows", "cols")),
        P(("rows", "cols")),
        P(("rows", "cols")),
    )
    out_specs = (P("rows", "cols"), P("rows", "cols"))
    return jax.shard_map(body, mesh=mesh, in_specs=in_specs, out_specs=out_specs, check_vma=False)
```

profile of v0, /device:TPU:12, one launch (start us, length us, event | category | flops | bytes accessed | tf_op | source)
XLA Modules:
  0.0 319.6 jit_solution(9164491619160554572)
XLA Ops:
  1.6 1.9 collective-permute-start
  3.7 4.5 %collective-permute-start.1 = (f32[5,512]{0,1:T(8,128)S(1)}, f32[5,512]{0,1:T(8,128)S(1)}, u32[]{:S(2)}, u32[]{:S(2)}) collective-permute-start(f32[5,512]{0,1:T(8,128)S(1)} %copy.142), channel_id=1, source_target_pairs={{4,0},{8,4},{12,8},{16,12},{20,16},{24,20},{28,24},{5,1},{9,5},{13... | collective-permute-start | bytes 30728 | tf_op jit(solution)/shard_map/ppermute | solution.py:18
  9.1 1.9 collective-permute-start.6
  11.2 4.5 %collective-permute-start.7 = (f32[4,512]{0,1:T(8,128)S(1)}, f32[4,512]{0,1:T(8,128)S(1)}, u32[]{:S(2)}, u32[]{:S(2)}) collective-permute-start(f32[4,512]{0,1:T(8,128)S(1)} %copy.149), channel_id=1, source_target_pairs={{4,0},{8,4},{12,8},{16,12},{20,16},{24,20},{28,24},{5,1},{9,5},{13... | collective-permute-start | bytes 24584 | tf_op jit(solution)/shard_map/ppermute | solution.py:18
  19.6 5.3 %all-to-all-start = ((s32[3,32,128]{2,0,1:T(4,128)}), s32[3,32,128]{2,0,1:T(4,128)S(1)}, u32[]{:S(2)}, u32[]{:S(2)}) async-start(s32[3,32,128]{2,0,1:T(4,128)} %copy.145), calls=%async_computation | async-start | bytes 131072 | tf_op jit(solution)/shard_map/all_to_all | solution.py:66
  27.3 3.4 %collective-permute-start.2 = (f32[138,5]{0,1:T(8,128)S(1)}, f32[138,5]{0,1:T(8,128)S(1)}, u32[]{:S(2)}, u32[]{:S(2)}) collective-permute-start(f32[138,5]{0,1:T(8,128)S(1)} %get-tuple-element.733), channel_id=1, source_target_pairs={{0,1},{1,2},{2,3},{4,5},{5,6},{6,7},{8,9},{9,10},{10,11},{12,13},{... | collective-permute-start | bytes 8288 | tf_op jit(solution)/shard_map/ppermute | solution.py:17
  30.7 2.5 collective-permute-start.3
  33.3 3.4 %collective-permute-start.8 = (f32[136,4]{0,1:T(4,128)S(1)}, f32[136,4]{0,1:T(4,128)S(1)}, u32[]{:S(2)}, u32[]{:S(2)}) collective-permute-start(f32[136,4]{0,1:T(4,128)S(1)} %get-tuple-element.731), channel_id=1, source_target_pairs={{0,1},{1,2},{2,3},{4,5},{5,6},{6,7},{8,9},{9,10},{10,11},{12,13},{... | collective-permute-start | bytes 6536 | tf_op jit(solution)/shard_map/ppermute | solution.py:17
  36.6 2.5 collective-permute-start.9
  39.4 2.7 collective-permute-done.9
  46.4 20.8 %while.60 = (s32[]{:T(128)}, f32[8,4,512]{2,1,0:T(4,128)S(1)}, s32[8,512]{1,0:T(8,128)}, s32[8,512]{1,0:T(8,128)}, f32[130,514]{1,0:T(8,128)S(1)}, /*index=5*/s32[]{:T(128)}) while((s32[]{:T(128)}, f32[8,4,512]{2,1,0:T(4,128)S(1)}, s32[8,512]{1,0:T(8,128)}, s32[8,512]{1,0:T(8,128)}, f32[130,514]{1,0:T(8,128)S(1)}, ...), condition=%wide.region_6.7_spmd.clone.clone, body=%wide.region_1.6_spmd.clone.clone.sunk | while | flops 823987200 | bytes 4793437 | solution.py:109
  68.5 4.2 %all-to-all-start.1 = ((f32[3,32,3,128]{3,0,2,1:T(4,128)}), f32[3,32,3,128]{3,0,2,1:T(4,128)S(1)}, u32[]{:S(2)}, u32[]{:S(2)}) async-start(f32[3,32,3,128]{3,0,2,1:T(4,128)} %copy.152), calls=%async_computation.1 | async-start | bytes 393216 | tf_op jit(solution)/shard_map/all_to_all | solution.py:75
  72.7 1.9 collective-permute-start.4
  74.6 2.4 collective-permute-start.5
  78.5 2.8 collective-permute-start.10
  81.2 1.9 collective-permute-start.11
  83.2 4.3 %collective-permute-done.11 = f32[32,3,128]{2,0,1:T(8,128)S(1)} collective-permute-done((f32[32,3,128]{2,0,1:T(8,128)S(1)}, f32[32,3,128]{2,0,1:T(8,128)S(1)}, u32[]{:S(2)}, u32[]{:S(2)}) %collective-permute-start.11) | collective-permute-done | bytes 49184 | tf_op jit(solution)/shard_map/ppermute | solution.py:26
  87.6 47.6 %while.62 = (s32[]{:T(128)}, f32[129,513]{1,0:T(8,128)S(1)}, s32[24,512]{1,0:T(8,128)S(1)}, f32[24,512]{1,0:T(8,128)S(1)}, f32[24,512]{1,0:T(8,128)S(1)}, /*index=5*/f32[24,512]{1,0:T(8,128)S(1)}, s32[]{:T(128)}, s32[]{:T(128)}) while((s32[]{:T(128)}, f32[129,513]{1,0:T(8,128)S(1)}, s32[24,512]{1,0:T(8,128)S(1)}, ...), condition=%wide.region_9.10_spmd.clone.clone, body=%wide.region_8.9_spmd.clone.clone.sunk | while | flops 408380160 | bytes 584819 | solution.py:156
  87.8 1.9 fusion.196
  91.7 1.9 fusion.196
  97.7 1.9 fusion.196
  103.6 1.9 fusion.196
  107.6 1.9 fusion.196
  109.6 1.9 fusion.196
  113.6 1.9 fusion.196
  115.5 1.9 fusion.196
  135.6 2.1 collective-permute-start.12
  137.8 3.7 %collective-permute-done.12 = f32[513]{0:T(1024)S(1)} collective-permute-done((f32[513]{0:T(1024)S(1)}, f32[513]{0:T(1024)S(1)}, u32[]{:S(2)}, u32[]{:S(2)}) %collective-permute-start.12) | collective-permute-done | bytes 2084 | tf_op jit(solution)/shard_map/ppermute | solution.py:26
  143.4 2.0 scatter-add.29
  145.3 3.4 %collective-permute-start.13 = (f32[128]{0:T(128)S(1)}, f32[128]{0:T(128)S(1)}, u32[]{:S(2)}, u32[]{:S(2)}) collective-permute-start(f32[128]{0:T(128)S(1)} %slice_bitcast_fusion.1), channel_id=1, source_target_pairs={{0,1},{1,2},{2,3},{4,5},{5,6},{6,7},{8,9},{9,10},{10,11},{12,13},{... | collective-permute-start | bytes 1544 | tf_op jit(solution)/shard_map/ppermute | solution.py:26
  149.3 38.9 %psum.7 = f32[]{:T(128)} all-reduce(f32[]{:T(128)} %reduce_sum.101), channel_id=1, replica_groups=mesh['rows'=8,'cols'=4] {'rows','cols'}, use_global_device_ids=true, to_apply=%region_12.13 | all-reduce | flops 1 | bytes 8 | tf_op jit(solution)/shard_map/psum | solution.py:192
  190.5 1.9 collective-permute-start.14
  192.4 4.5 %collective-permute-start.15 = (f32[4,512]{0,1:T(8,128)S(1)}, f32[4,512]{0,1:T(8,128)S(1)}, u32[]{:S(2)}, u32[]{:S(2)}) collective-permute-start(f32[4,512]{0,1:T(8,128)S(1)} %get-tuple-element.736), channel_id=1, source_target_pairs={{4,0},{8,4},{12,8},{16,12},{20,16},{24,20},{28,24},{5,1},{9,5},{13... | collective-permute-start | bytes 24584 | tf_op jit(solution)/shard_map/ppermute | solution.py:18
  197.0 2.3 collective-permute-done.14
  200.9 2.8 collective-permute-start.16
  203.7 3.0 collective-permute-start.17
  206.8 2.5 collective-permute-done.17
  213.0 20.8 %while.61 = (s32[]{:T(128)}, f32[8,4,512]{2,1,0:T(4,128)S(1)}, s32[8,512]{1,0:T(8,128)}, s32[8,512]{1,0:T(8,128)}, f32[130,514]{1,0:T(8,128)S(1)}, /*index=5*/s32[]{:T(128)}) while((s32[]{:T(128)}, f32[8,4,512]{2,1,0:T(4,128)S(1)}, s32[8,512]{1,0:T(8,128)}, s32[8,512]{1,0:T(8,128)}, f32[130,514]{1,0:T(8,128)S(1)}, ...), condition=%wide.region_18.19_spmd.clone.clone, body=%wide.region_13.18_spmd.clone.clone.sunk | while | flops 823987200 | bytes 4793437 | solution.py:109
  234.4 10.7 %all_to_all.15 = f32[3,32,3,128]{3,0,2,1:T(4,128)S(1)} all-to-all(f32[3,32,3,128]{3,0,2,1:T(4,128)S(1)} %copy.161), channel_id=1, replica_groups=mesh['rows'=8,'cols'=4] {'cols'}, dimensions={1} | all-to-all | bytes 294912 | tf_op jit(solution)/shard_map/all_to_all | solution.py:75
  245.2 3.2 %collective-permute-start.18 = (f32[32,3,128]{2,0,1:T(8,128)S(1)}, f32[32,3,128]{2,0,1:T(8,128)S(1)}, u32[]{:S(2)}, u32[]{:S(2)}) collective-permute-start(f32[32,3,128]{2,0,1:T(8,128)S(1)} %bitcast.255), channel_id=1, source_target_pairs={{4,0},{8,4},{12,8},{16,12},{20,16},{24,20},{28,24},{5,1},{9,5},{13... | collective-permute-start | bytes 147464 | tf_op jit(solution)/shard_map/ppermute | solution.py:26
  248.4 1.9 collective-permute-start.19
  250.4 4.3 %collective-permute-done.19 = f32[32,3,128]{2,0,1:T(8,128)S(1)} collective-permute-done((f32[32,3,128]{2,0,1:T(8,128)S(1)}, f32[32,3,128]{2,0,1:T(8,128)S(1)}, u32[]{:S(2)}, u32[]{:S(2)}) %collective-permute-start.19) | collective-permute-done | bytes 49184 | tf_op jit(solution)/shard_map/ppermute | solution.py:26
  254.8 47.6 %while.63 = (s32[]{:T(128)}, f32[129,513]{1,0:T(8,128)S(1)}, s32[24,512]{1,0:T(8,128)S(1)}, f32[24,512]{1,0:T(8,128)S(1)}, f32[24,512]{1,0:T(8,128)S(1)}, /*index=5*/f32[24,512]{1,0:T(8,128)S(1)}, s32[]{:T(128)}, s32[]{:T(128)}) while((s32[]{:T(128)}, f32[129,513]{1,0:T(8,128)S(1)}, s32[24,512]{1,0:T(8,128)S(1)}, ...), condition=%wide.region_20.21_spmd.clone.clone, body=%wide.region_19.20_spmd.clone.clone.sunk | while | flops 408380160 | bytes 584819 | solution.py:156
  302.8 1.9 collective-permute-start.20
  304.8 3.9 %collective-permute-done.20 = f32[513]{0:T(1024)S(1)} collective-permute-done((f32[513]{0:T(1024)S(1)}, f32[513]{0:T(1024)S(1)}, u32[]{:S(2)}, u32[]{:S(2)}) %collective-permute-start.20) | collective-permute-done | bytes 2084 | tf_op jit(solution)/shard_map/ppermute | solution.py:26
  310.5 2.0 scatter-add.35
  312.5 2.3 collective-permute-start.21
  315.8 2.2 collective-permute-done.21
  (588 shorter events, 148.6 us)
Async XLA Ops:
  0.6 25.1 %copy-start = (f32[128,512]{1,0:T(8,128)S(1)}, f32[128,512]{1,0:T(8,128)}, u32[]{:S(2)}) copy-start(f32[128,512]{1,0:T(8,128)} %param.31) | copy-start | bytes 786436
  0.6 25.2 %copy-start.1 = (f32[128,512]{1,0:T(8,128)S(1)}, f32[128,512]{1,0:T(8,128)}, u32[]{:S(2)}) copy-start(f32[128,512]{1,0:T(8,128)} %param.32) | copy-start | bytes 786436
  0.7 24.3 %copy-start.5 = (f32[2,4096]{1,0:T(2,128)S(1)}, f32[2,4096]{1,0:T(2,128)}, u32[]{:S(2)}) copy-start(f32[2,4096]{1,0:T(2,128)} %param.34) | copy-start | bytes 98308
  0.7 25.0 %copy-start.6 = (s32[4096]{0:T(1024)S(1)}, s32[4096]{0:T(1024)}, u32[]{:S(2)}) copy-start(s32[4096]{0:T(1024)} %param.33) | copy-start | bytes 49156
  1.6 25.6 %collective-permute-start = (f32[5,512]{0,1:T(8,128)S(1)}, f32[5,512]{0,1:T(8,128)S(1)}, u32[]{:S(2)}, u32[]{:S(2)}) collective-permute-start(f32[5,512]{0,1:T(8,128)S(1)} %copy.141), channel_id=1, source_target_pairs={{0,4},{4,8},{8,12},{12,16},{16,20},{20,24},{24,28},{1,5},{5,9},{9,... | collective-permute-start | bytes 30728 | tf_op jit(solution)/shard_map/ppermute | solution.py:17
  3.7 23.5 %collective-permute-start.1 = (f32[5,512]{0,1:T(8,128)S(1)}, f32[5,512]{0,1:T(8,128)S(1)}, u32[]{:S(2)}, u32[]{:S(2)}) collective-permute-start(f32[5,512]{0,1:T(8,128)S(1)} %copy.142), channel_id=1, source_target_pairs={{4,0},{8,4},{12,8},{16,12},{20,16},{24,20},{28,24},{5,1},{9,5},{13... | collective-permute-start | bytes 30728 | tf_op jit(solution)/shard_map/ppermute | solution.py:18
  9.1 24.0 %collective-permute-start.6 = (f32[4,512]{0,1:T(8,128)S(1)}, f32[4,512]{0,1:T(8,128)S(1)}, u32[]{:S(2)}, u32[]{:S(2)}) collective-permute-start(f32[4,512]{0,1:T(8,128)S(1)} %copy.148), channel_id=1, source_target_pairs={{0,4},{4,8},{8,12},{12,16},{16,20},{20,24},{24,28},{1,5},{5,9},{9,... | collective-permute-start | bytes 24584 | tf_op jit(solution)/shard_map/ppermute | solution.py:17
  11.2 22.0 %collective-permute-start.7 = (f32[4,512]{0,1:T(8,128)S(1)}, f32[4,512]{0,1:T(8,128)S(1)}, u32[]{:S(2)}, u32[]{:S(2)}) collective-permute-start(f32[4,512]{0,1:T(8,128)S(1)} %copy.149), channel_id=1, source_target_pairs={{4,0},{8,4},{12,8},{16,12},{20,16},{24,20},{28,24},{5,1},{9,5},{13... | collective-permute-start | bytes 24584 | tf_op jit(solution)/shard_map/ppermute | solution.py:18
  19.6 48.9 %all-to-all-start = ((s32[3,32,128]{2,0,1:T(4,128)}), s32[3,32,128]{2,0,1:T(4,128)S(1)}, u32[]{:S(2)}, u32[]{:S(2)}) async-start(s32[3,32,128]{2,0,1:T(4,128)} %copy.145), calls=%async_computation | async-start | bytes 131072 | tf_op jit(solution)/shard_map/all_to_all | solution.py:66
  27.3 11.8 %collective-permute-start.2 = (f32[138,5]{0,1:T(8,128)S(1)}, f32[138,5]{0,1:T(8,128)S(1)}, u32[]{:S(2)}, u32[]{:S(2)}) collective-permute-start(f32[138,5]{0,1:T(8,128)S(1)} %get-tuple-element.733), channel_id=1, source_target_pairs={{0,1},{1,2},{2,3},{4,5},{5,6},{6,7},{8,9},{9,10},{10,11},{12,13},{... | collective-permute-start | bytes 8288 | tf_op jit(solution)/shard_map/ppermute | solution.py:17
  30.7 8.4 %collective-permute-start.3 = (f32[138,5]{0,1:T(8,128)S(1)}, f32[138,5]{0,1:T(8,128)S(1)}, u32[]{:S(2)}, u32[]{:S(2)}) collective-permute-start(f32[138,5]{0,1:T(8,128)S(1)} %get-tuple-element.734), channel_id=1, source_target_pairs={{1,0},{2,1},{3,2},{5,4},{6,5},{7,6},{9,8},{10,9},{11,10},{13,12},{... | collective-permute-start | bytes 8288 | tf_op jit(solution)/shard_map/ppermute | solution.py:18
  33.3 6.1 %collective-permute-start.8 = (f32[136,4]{0,1:T(4,128)S(1)}, f32[136,4]{0,1:T(4,128)S(1)}, u32[]{:S(2)}, u32[]{:S(2)}) collective-permute-start(f32[136,4]{0,1:T(4,128)S(1)} %get-tuple-element.731), channel_id=1, source_target_pairs={{0,1},{1,2},{2,3},{4,5},{5,6},{6,7},{8,9},{9,10},{10,11},{12,13},{... | collective-permute-start | bytes 6536 | tf_op jit(solution)/shard_map/ppermute | solution.py:17
  36.6 5.5 %collective-permute-start.9 = (f32[136,4]{0,1:T(4,128)S(1)}, f32[136,4]{0,1:T(4,128)S(1)}, u32[]{:S(2)}, u32[]{:S(2)}) collective-permute-start(f32[136,4]{0,1:T(4,128)S(1)} %get-tuple-element.732), channel_id=1, source_target_pairs={{1,0},{2,1},{3,2},{5,4},{6,5},{7,6},{9,8},{10,9},{11,10},{13,12},{... | collective-permute-start | bytes 6536 | tf_op jit(solution)/shard_map/ppermute | solution.py:18
  46.3 21.0 %copy-start.3 = (f32[1,4096]{1,0:T(1,128)S(1)}, f32[1,4096]{1,0:T(1,128)}, u32[]{:S(2)}) copy-start(f32[1,4096]{1,0:T(1,128)} %get-tuple-element.768) | copy-start | bytes 49156
  46.3 20.9 %copy-start.4 = (f32[1,4096]{1,0:T(1,128)S(1)}, f32[1,4096]{1,0:T(1,128)}, u32[]{:S(2)}) copy-start(f32[1,4096]{1,0:T(1,128)} %get-tuple-element.769) | copy-start | bytes 49156
  46.3 21.0 %copy-start.2 = (f32[4096]{0:T(1024)S(1)}, f32[4096]{0:T(1024)}, u32[]{:S(2)}) copy-start(f32[4096]{0:T(1024)} %param.35) | copy-start | bytes 49156
  68.5 9.9 %all-to-all-start.1 = ((f32[3,32,3,128]{3,0,2,1:T(4,128)}), f32[3,32,3,128]{3,0,2,1:T(4,128)S(1)}, u32[]{:S(2)}, u32[]{:S(2)}) async-start(f32[3,32,3,128]{3,0,2,1:T(4,128)} %copy.152), calls=%async_computation.1 | async-start | bytes 393216 | tf_op jit(solution)/shard_map/all_to_all | solution.py:75
  72.7 10.5 %collective-permute-start.4 = (s32[32,128]{1,0:T(8,128)S(1)}, s32[32,128]{1,0:T(8,128)S(1)}, u32[]{:S(2)}, u32[]{:S(2)}) collective-permute-start(s32[32,128]{1,0:T(8,128)S(1)} %bitcast.259), channel_id=1, source_target_pairs={{4,0},{8,4},{12,8},{16,12},{20,16},{24,20},{28,24},{5,1},{9,5},{13... | collective-permute-start | bytes 49160 | tf_op jit(solution)/shard_map/ppermute | solution.py:26
  74.6 8.6 %collective-permute-start.5 = (s32[32,128]{1,0:T(8,128)S(1)}, s32[32,128]{1,0:T(8,128)S(1)}, u32[]{:S(2)}, u32[]{:S(2)}) collective-permute-start(s32[32,128]{1,0:T(8,128)S(1)} %bitcast.258), channel_id=1, source_target_pairs={{0,4},{4,8},{8,12},{12,16},{16,20},{20,24},{24,28},{1,5},{5,9},{9,... | collective-permute-start | bytes 49160 | tf_op jit(solution)/shard_map/ppermute | solution.py:26
  78.5 4.8 %collective-permute-start.10 = (f32[32,3,128]{2,0,1:T(8,128)S(1)}, f32[32,3,128]{2,0,1:T(8,128)S(1)}, u32[]{:S(2)}, u32[]{:S(2)}) collective-permute-start(f32[32,3,128]{2,0,1:T(8,128)S(1)} %bitcast.253), channel_id=1, source_target_pairs={{4,0},{8,4},{12,8},{16,12},{20,16},{24,20},{28,24},{5,1},{9,5},{13... | collective-permute-start | bytes 147464 | tf_op jit(solution)/shard_map/ppermute | solution.py:26
  81.2 6.3 %collective-permute-start.11 = (f32[32,3,128]{2,0,1:T(8,128)S(1)}, f32[32,3,128]{2,0,1:T(8,128)S(1)}, u32[]{:S(2)}, u32[]{:S(2)}) collective-permute-start(f32[32,3,128]{2,0,1:T(8,128)S(1)} %bitcast.254), channel_id=1, source_target_pairs={{0,4},{4,8},{8,12},{12,16},{16,20},{20,24},{24,28},{1,5},{5,9},{9,... | collective-permute-start | bytes 147464 | tf_op jit(solution)/shard_map/ppermute | solution.py:26
  135.6 5.8 %collective-permute-start.12 = (f32[513]{0:T(1024)S(1)}, f32[513]{0:T(1024)S(1)}, u32[]{:S(2)}, u32[]{:S(2)}) collective-permute-start(f32[513]{0:T(1024)S(1)} %slice_reduce_fusion.1), channel_id=1, source_target_pairs={{0,4},{4,8},{8,12},{12,16},{16,20},{20,24},{24,28},{1,5},{5,9},{9,... | collective-permute-start | bytes 6164 | tf_op jit(solution)/shard_map/ppermute | solution.py:26
  145.3 44.2 %collective-permute-start.13 = (f32[128]{0:T(128)S(1)}, f32[128]{0:T(128)S(1)}, u32[]{:S(2)}, u32[]{:S(2)}) collective-permute-start(f32[128]{0:T(128)S(1)} %slice_bitcast_fusion.1), channel_id=1, source_target_pairs={{0,1},{1,2},{2,3},{4,5},{5,6},{6,7},{8,9},{9,10},{10,11},{12,13},{... | collective-permute-start | bytes 1544 | tf_op jit(solution)/shard_map/ppermute | solution.py:26
  190.5 8.8 %collective-permute-start.14 = (f32[4,512]{0,1:T(8,128)S(1)}, f32[4,512]{0,1:T(8,128)S(1)}, u32[]{:S(2)}, u32[]{:S(2)}) collective-permute-start(f32[4,512]{0,1:T(8,128)S(1)} %get-tuple-element.735), channel_id=1, source_target_pairs={{0,4},{4,8},{8,12},{12,16},{16,20},{20,24},{24,28},{1,5},{5,9},{9,... | collective-permute-start | bytes 24584 | tf_op jit(solution)/shard_map/ppermute | solution.py:17
  192.4 8.4 %collective-permute-start.15 = (f32[4,512]{0,1:T(8,128)S(1)}, f32[4,512]{0,1:T(8,128)S(1)}, u32[]{:S(2)}, u32[]{:S(2)}) collective-permute-start(f32[4,512]{0,1:T(8,128)S(1)} %get-tuple-element.736), channel_id=1, source_target_pairs={{4,0},{8,4},{12,8},{16,12},{20,16},{24,20},{28,24},{5,1},{9,5},{13... | collective-permute-start | bytes 24584 | tf_op jit(solution)/shard_map/ppermute | solution.py:18
  200.9 5.8 %collective-permute-start.16 = (f32[136,4]{0,1:T(4,128)S(1)}, f32[136,4]{0,1:T(4,128)S(1)}, u32[]{:S(2)}, u32[]{:S(2)}) collective-permute-start(f32[136,4]{0,1:T(4,128)S(1)} %get-tuple-element.729), channel_id=1, source_target_pairs={{0,1},{1,2},{2,3},{4,5},{5,6},{6,7},{8,9},{9,10},{10,11},{12,13},{... | collective-permute-start | bytes 6536 | tf_op jit(solution)/shard_map/ppermute | solution.py:17
  203.7 5.6 %collective-permute-start.17 = (f32[136,4]{0,1:T(4,128)S(1)}, f32[136,4]{0,1:T(4,128)S(1)}, u32[]{:S(2)}, u32[]{:S(2)}) collective-permute-start(f32[136,4]{0,1:T(4,128)S(1)} %get-tuple-element.730), channel_id=1, source_target_pairs={{1,0},{2,1},{3,2},{5,4},{6,5},{7,6},{9,8},{10,9},{11,10},{13,12},{... | collective-permute-start | bytes 6536 | tf_op jit(solution)/shard_map/ppermute | solution.py:18
  245.2 5.2 %collective-permute-start.18 = (f32[32,3,128]{2,0,1:T(8,128)S(1)}, f32[32,3,128]{2,0,1:T(8,128)S(1)}, u32[]{:S(2)}, u32[]{:S(2)}) collective-permute-start(f32[32,3,128]{2,0,1:T(8,128)S(1)} %bitcast.255), channel_id=1, source_target_pairs={{4,0},{8,4},{12,8},{16,12},{20,16},{24,20},{28,24},{5,1},{9,5},{13... | collective-permute-start | bytes 147464 | tf_op jit(solution)/shard_map/ppermute | solution.py:26
  248.4 6.3 %collective-permute-start.19 = (f32[32,3,128]{2,0,1:T(8,128)S(1)}, f32[32,3,128]{2,0,1:T(8,128)S(1)}, u32[]{:S(2)}, u32[]{:S(2)}) collective-permute-start(f32[32,3,128]{2,0,1:T(8,128)S(1)} %bitcast.256), channel_id=1, source_target_pairs={{0,4},{4,8},{8,12},{12,16},{16,20},{20,24},{24,28},{1,5},{5,9},{9,... | collective-permute-start | bytes 147464 | tf_op jit(solution)/shard_map/ppermute | solution.py:26
  302.8 5.8 %collective-permute-start.20 = (f32[513]{0:T(1024)S(1)}, f32[513]{0:T(1024)S(1)}, u32[]{:S(2)}, u32[]{:S(2)}) collective-permute-start(f32[513]{0:T(1024)S(1)} %slice_reduce_fusion), channel_id=1, source_target_pairs={{0,4},{4,8},{8,12},{12,16},{16,20},{20,24},{24,28},{1,5},{5,9},{9,... | collective-permute-start | bytes 6164 | tf_op jit(solution)/shard_map/ppermute | solution.py:26
  312.5 5.5 %collective-permute-start.21 = (f32[128]{0:T(128)S(1)}, f32[128]{0:T(128)S(1)}, u32[]{:S(2)}, u32[]{:S(2)}) collective-permute-start(f32[128]{0:T(128)S(1)} %slice_bitcast_fusion), channel_id=1, source_target_pairs={{0,1},{1,2},{2,3},{4,5},{5,6},{6,7},{8,9},{9,10},{10,11},{12,13},{... | collective-permute-start | bytes 1544 | tf_op jit(solution)/shard_map/ppermute | solution.py:26
where the time goes:
time: 324 us; the launch traced here: 320 us
  matrix products  107 us (33%)
  starting transfers between devices  70.2 us (22%)
  blocking collectives  49.6 us (15%)
  local copies, waits for them, and re-layouts  30.6 us (9%)
  waiting for transfers between devices  28.8 us (9%)
  other arithmetic  27.1 us (8%)
  loops' own time  4.26 us (1%)
    dot_general x48, matrix products, step(): lax.dot_general(row_side, col_side, (((0,), (0,)), ((), ())), precision=l...  89 us
    psum x1, blocking collectives, body(): total = lax.psum(jnp.sum(weights), ('rows', 'cols'))  38.9 us
    ppermute x10, starting transfers between devices, from_behind(): lax.ppermute(value, axis, [(source, source + steps) for source in range(i...  23.8 us
    ppermute x6, starting transfers between devices, padded_2(): after = lax.ppermute(initial, axis, down)  21.6 us
    ppermute x10, waiting for transfers between devices, from_behind(): lax.ppermute(value, axis, [(source, source + steps) for source in range(i...  18.4 us
    dot_general x16, matrix products, step(): jnp.dot(picks, padded, precision=lax.Precision.HIGHEST, preferred_element...  17.2 us
    ppermute x6, starting transfers between devices, padded_2(): before = lax.ppermute(last, axis, up)  15.3 us
    dynamic_slice x16, local copies, waits for them, and re-layouts, sample_corners(): lax.scan(step, jnp.zeros((), jnp.float32), (row_top, col_left))  11.9 us
  transfers between devices with their start and end apart: 24, of which 10 were waited for; matrix products, arithmetic and copies ran while one was open for 11% of the time, Pallas kernels for 0%

commit v1 on v0

v1 whole, which is shorter than its diff:
```python
import functools
import jax
import jax.numpy as jnp
from jax import lax
from jax.experimental import pallas as pl
from jax.experimental.pallas import tpu as pltpu
from jax.sharding import PartitionSpec as P

HJB_STEPS = 4
ITERS = 2
F32, BF16, I32 = jnp.float32, jnp.bfloat16, jnp.int32

PAD = 16
EDGE = 8
GROUP = 8


def swap_pairs(count):
    first = [(i, i ^ 1) for i in range(count)]
    second = [(i, ((i + 1) ^ 1) - 1) for i in range(1, count - 1)]
    return first, second


def swap_both(first, second, axis):
    pairs_a, pairs_b = swap_pairs(lax.axis_size(axis))
    return lax.ppermute(first, axis, pairs_a), lax.ppermute(second, axis, pairs_b)


def xor_permute(value, axis, bit):
    return lax.ppermute(value, axis, [(i, i ^ bit) for i in range(lax.axis_size(axis))])


def vmem_call(kernel, out_shape, n_in, scratch=(), smem_in=()):
    in_specs = [
        pl.BlockSpec(memory_space=pltpu.SMEM if i in smem_in else pltpu.VMEM) for i in range(n_in)
    ]
    return pl.pallas_call(
        kernel,
        out_shape=out_shape,
        in_specs=in_specs,
        out_specs=jax.tree.map(lambda _: pl.BlockSpec(memory_space=pltpu.VMEM), out_shape),
        scratch_shapes=list(scratch),
    )


def shape(*dims, dtype=F32):
    return jax.ShapeDtypeStruct(dims, dtype)


def flipped(block):
    rows = block.shape[0]
    width = -(-rows // 128) * 128
    if width > rows:
        block = jnp.concatenate([block, jnp.zeros((width - rows, 128), F32)], axis=0)
    parts = [block[i : i + 128].T for i in range(0, width, 128)]
    return jnp.concatenate(parts, axis=1)


def unflipped(block, rows):
    parts = [block[:, i : i + 128].T for i in range(0, block.shape[1], 128)]
    return jnp.concatenate(parts, axis=0)[:rows]


def pick(flag, one, other):
    return jnp.where(flag, one, other)


def start_mid_kernel(rows, cols, u_ref, m_ref, a_ref, b_ref, ue_ref, me_ref, ca_ref, cb_ref):
    row_even = lax.axis_index("rows") % 2 == 0
    col_even = lax.axis_index("cols") % 2 == 0
    for index, (src, dst) in enumerate(((u_ref, ue_ref), (m_ref, me_ref))):
        dst[...] = jnp.zeros(dst.shape, F32)
        dst[PAD : PAD + rows, 0:cols] = src[...]
        part = slice(index * EDGE, (index + 1) * EDGE)
        north = pick(row_even, b_ref[part, :], a_ref[part, :])
        south = pick(row_even, a_ref[part, :], b_ref[part, :])
        dst[PAD - EDGE : PAD, 0:cols] = north
        dst[PAD + rows : PAD + rows + EDGE, 0:cols] = south
        west_going = flipped(dst[:, 0:128])[0:EDGE]
        east_going = flipped(dst[:, cols - 128 : cols])[128 - EDGE : 128]
        ca_ref[part, :] = pick(col_even, east_going, west_going)
        cb_ref[part, :] = pick(col_even, west_going, east_going)


def side_tile(left, right, width):
    return jnp.concatenate([right, jnp.zeros((128 - 2 * EDGE, width), F32), left], axis=0)


def hjb_sweep(rows, cols, ua, ub, m):
    wide = cols + 128
    n_rows, n_cols = lax.axis_size("rows"), lax.axis_size("cols")
    lane = lax.broadcasted_iota(I32, (8, wide), 1)
    col = jnp.where(lane < cols + 64, lane, lane - wide) + lax.axis_index("cols") * cols
    col_ok = (col >= 0) & (col < cols * n_cols)
    sub = lax.broadcasted_iota(I32, (8, wide), 0)
    row_first = lax.axis_index("rows") * rows
    src, dst = ua, ub
    for step in range(HJB_STEPS):
        for i in range(PAD - 8, PAD + rows + 8, 8):
            value = src[i : i + 8, :]
            up = src[i - 1 : i + 7, :]
            down = src[i + 1 : i + 9, :]
            left = pltpu.roll(value, 1, 1)
            right = pltpu.roll(value, wide - 1, 1)
            back_x = jnp.maximum(value - up, 0.0)
            fore_x = jnp.minimum(down - value, 0.0)
            back_y = jnp.maximum(value - left, 0.0)
            fore_y = jnp.minimum(right - value, 0.0)
            square_x = jnp.maximum(back_x * back_x, fore_x * fore_x)
            square_y = jnp.maximum(back_y * back_y, fore_y * fore_y)
            spread = up + down + left + right - 4.0 * value
            update = 0.5 * spread - 0.5 * (square_x + square_y) + 0.5 * m[i : i + 8, :]
            ok = col_ok
            if i < PAD or i >= PAD + rows:
                row = sub + (row_first + (i - PAD))
                ok = ok & (row >= 0) & (row < rows * n_rows)
            dst[i : i + 8, :] = jnp.where(ok, value + 0.25 * update, 0.0)
        src, dst = dst, src
    return src


def split(value):
    high = value.astype(BF16)
    return high, (value - high.astype(F32)).astype(BF16)


def fill_tables(rows, cols, u, tab):
    wide = cols + 128
    for i in range(0, rows, 16):
        here = u[PAD + i : PAD + i + 16, :]
        below = u[PAD + i + 1 : PAD + i + 17, :]
        d_x = below - here
        d_y = pltpu.roll(here, wide - 1, 1) - here
        d_xy = pltpu.roll(d_x, wide - 1, 1) - d_x
        for index, table in enumerate((d_x, d_y, d_xy)):
            high, low = split(table[:, 0:cols])
            tab[index * rows + i : index * rows + i + 16, :] = high
            tab[(3 + index) * rows + i : (3 + index) * rows + i + 16, :] = low


def sample_moves(
    rows, cols, blocks, cap, first, tab, starts, offs, wts, ends, dest, buf, slot_row, counter
):
    n_cols = lax.axis_size("cols")
    my_row, my_col = lax.axis_index("rows"), lax.axis_index("cols")
    kinds = 4 if first else 2
    part_rows = 3 * kinds * cap + (EDGE if first else 0)
    buf[...] = jnp.zeros(buf.shape, F32)
    for i in range(3 * n_cols):
        counter[i] = 0
    for b in range(blocks):
        tile = dest[b]
        band, column = tile // n_cols, tile % n_cols
        section = jnp.where(band == my_row, 0, jnp.where(band == (my_row ^ 1), 1, 2))
        distance = column ^ my_col
        rank = counter[distance * 3 + section]
        counter[distance * 3 + section] = rank + 1
        slot_row[b] = distance * part_rows + section * (kinds * cap) + rank

    col_iota = lax.broadcasted_iota(I32, (cols, 256), 0)
    row_iota = lax.broadcasted_iota(I32, (rows, 256), 0)

    def step(j, carry):
        def pair(ref):
            return jnp.concatenate([ref[pl.ds(2 * j, 1), :], ref[pl.ds(2 * j + 1, 1), :]], axis=1)

        cell = pair(starts)
        row, col = cell // cols, cell % cols
        lanes = pl.ds(pl.multiple_of(j * 256, 256), 256)
        off_x = offs[0:1, lanes]
        off_y = offs[1:2, lanes]
        hot = jnp.where(col_iota == col, 1.0, 0.0).astype(BF16)
        lines = jnp.dot(tab[...], hot, preferred_element_type=F32)
        row_hit = row_iota == row
        found = []
        for index in range(3):
            line = (
                lines[index * rows : (index + 1) * rows]
                + lines[(3 + index) * rows : (4 + index) * rows]
            )
            found.append(jnp.sum(jnp.where(row_hit, line, 0.0), axis=0, keepdims=True))
        d_x, d_y, d_xy = found
        frac_x = 0.5 + 0.45 * jnp.tanh(off_x)
        frac_y = 0.5 + 0.45 * jnp.tanh(off_y)
        moved_x = 0.5 + 0.45 * jnp.tanh(off_x - (d_x + frac_y * d_xy))
        moved_y = 0.5 + 0.45 * jnp.tanh(off_y - (d_y + frac_x * d_xy))
        out = [moved_x, moved_y]
        if first:
            out += [pair(wts), (pair(ends) + 1).astype(F32)]
        for half in range(2):
            base = slot_row[2 * j + half]
            for q, value in enumerate(out):
                buf[pl.ds(base + q * cap, 1), :] = value[:, half * 128 : (half + 1) * 128]
        return carry

    lax.fori_loop(0, blocks // 2, step, 0)


def first_kernel(
    rows, cols, blocks, cap, n_cols, *refs
):
    (ue_in, me_in, ra_ref, rb_ref, starts, offs, wts, ends, dest) = refs[:9]
    outs = refs[9 : 9 + n_cols]
    ue_ref, me_ref = refs[9 + n_cols : 11 + n_cols]
    ua, ub, tab, buf, slot_row, counter = refs[11 + n_cols :]
    col_even = lax.axis_index("cols") % 2 == 0
    tall = ue_in.shape[0]
    width = ra_ref.shape[1]
    for index, (src, dst) in enumerate(((ue_in, ue_ref), (me_in, me_ref))):
        part = slice(index * EDGE, (index + 1) * EDGE)
        west = pick(col_even, rb_ref[part, :], ra_ref[part, :])
        east = pick(col_even, ra_ref[part, :], rb_ref[part, :])
        dst[:, 0:cols] = src[:, 0:cols]
        dst[:, cols : cols + 128] = unflipped(side_tile(west, east, width), tall)
    ua[...] = ue_ref[...]
    ub[...] = jnp.zeros(ub.shape, F32)
    u = hjb_sweep(rows, cols, ua, ub, me_ref)
    fill_tables(rows, cols, u, tab)
    sample_moves(
        rows, cols, blocks, cap, True, tab, starts, offs, wts, ends, dest, buf, slot_row, counter
    )
    part_rows = 12 * cap + EDGE
    total = jnp.sum(jnp.sum(wts[...], axis=0, keepdims=True), axis=1, keepdims=True)
    for k in range(n_cols):
        outs[k][0 : part_rows - EDGE, :] = buf[k * part_rows : (k + 1) * part_rows - EDGE, :]
        outs[k][part_rows - EDGE :, :] = jnp.broadcast_to(total, (EDGE, 128))


def again_kernel(rows, cols, blocks, cap, n_cols, *refs):
    (ue_ref, m_in, d_ref, ra_ref, rb_ref, total_ref, starts, offs, dest) = refs[:9]
    outs = refs[9 : 9 + n_cols]
    value_ref, density_ref = refs[9 + n_cols : 11 + n_cols]
    ua, ub, m, tab, buf, slot_row, counter = refs[11 + n_cols :]
    col_even = lax.axis_index("cols") % 2 == 0
    n_rows = lax.axis_size("rows")
    tall = ue_ref.shape[0]
    width = ra_ref.shape[1]
    half_scale = 0.5 * ((rows * cols * n_rows * n_cols) / total_ref[0:1, 0:1])
    west = pick(col_even, rb_ref[...], ra_ref[...])
    east = pick(col_even, ra_ref[...], rb_ref[...])
    side = unflipped(side_tile(west[0:EDGE], east[0:EDGE], width), tall)
    pushed = unflipped(
        jnp.concatenate([west[EDGE : 2 * EDGE], jnp.zeros((128 - EDGE, width), F32)], axis=0), tall
    )
    m[:, 0:128] = 0.5 * m_in[:, 0:128] + half_scale * (d_ref[:, 0:128] + pushed)
    m[:, 128:cols] = 0.5 * m_in[:, 128:cols] + half_scale * d_ref[:, 128:cols]
    m[:, cols : cols + 128] = 0.5 * m_in[:, cols : cols + 128] + half_scale * (
        d_ref[:, cols : cols + 128] + side
    )
    density_ref[...] = m[PAD : PAD + rows, 0:cols]
    ua[...] = ue_ref[...]
    ub[...] = jnp.zeros(ub.shape, F32)
    u = hjb_sweep(rows, cols, ua, ub, m)
    value_ref[...] = u[PAD : PAD + rows, 0:cols]
    fill_tables(rows, cols, u, tab)
    sample_moves(
        rows, cols, blocks, cap, False, tab, starts, offs, None, None, dest, buf, slot_row, counter
    )
    part_rows = 6 * cap
    for k in range(n_cols):
        outs[k][...] = buf[k * part_rows : (k + 1) * part_rows, :]


def deposit_grid(rows, cols, cap, chunks, moves, masses, acc, lhs, rhs, slots, grid):
    counts = []
    for q in range(chunks):
        cells = masses[(2 * q + 1) * cap : (2 * q + 2) * cap, :]
        counts.append(jnp.sum(jnp.where(cells > 0.5, 1.0, 0.0)).astype(I32) // 128)
    base = jnp.int32(0)
    for q in range(chunks):
        for rank in range(cap):
            slots[base + rank] = 2 * q * cap + rank
        base = base + counts[q]
    for rank in range(GROUP):
        slots[base + rank] = 2 * chunks * cap
    acc[...] = jnp.zeros(acc.shape, F32)
    row_iota = lax.broadcasted_iota(I32, (rows, 128), 0)
    spill_iota = lax.broadcasted_iota(I32, (16, 128), 0)
    col_iota = lax.broadcasted_iota(I32, (cols, 128), 0)

    def step(g, carry):
        for t in range(GROUP):
            at = slots[g * GROUP + t]
            move_x = moves[pl.ds(at, 1), :]
            move_y = moves[pl.ds(at + cap, 1), :]
            mass = masses[pl.ds(at, 1), :]
            cell = masses[pl.ds(at + cap, 1), :].astype(I32) - 1
            row, col = cell // cols, cell % cols
            stay, go = mass * (1.0 - move_x), mass * move_x
            parts = []
            for factor in (1.0 - move_y, move_y):
                parts.append((split(stay * factor), split(go * factor)))
            lanes = slice(t * 128, (t + 1) * 128)
            here, next_row = row_iota == row, row_iota == row + 1
            last = row == rows - 1
            spill = jnp.zeros((16, 128), F32)
            for side in range(2):
                (stay_pair, go_pair) = parts[side]
                for level in range(2):
                    index = 2 * side + level
                    first, second = stay_pair[level].astype(F32), go_pair[level].astype(F32)
                    lhs[index * rows : (index + 1) * rows, lanes] = jnp.where(
                        here, first, jnp.where(next_row, second, 0.0)
                    ).astype(BF16)
                    spill = jnp.where((spill_iota == index) & last, second, spill)
            lhs[4 * rows : 4 * rows + 16, lanes] = spill.astype(BF16)
            rhs[:, lanes] = jnp.where(col_iota == col, 1.0, 0.0).astype(BF16)
        acc[...] += lax.dot_general(
            lhs[...], rhs[...], (((1,), (1,)), ((), ())), preferred_element_type=F32
        )
        return carry

    lax.fori_loop(0, (base + GROUP - 1) // GROUP, step, 0)

    wide = cols + 128
    lane = lax.broadcasted_iota(I32, (8, wide), 1)

    def join(stay, pushed):
        blank = jnp.zeros((8, 128), F32)
        stay = jnp.concatenate([stay, blank], axis=1)
        pushed = jnp.concatenate([pushed, blank], axis=1)
        return stay + pltpu.roll(pushed, 1, 1)

    for i in range(0, rows, 8):
        grid[i : i + 8, :] = join(
            acc[i : i + 8, :] + acc[rows + i : rows + i + 8, :],
            acc[2 * rows + i : 2 * rows + i + 8, :] + acc[3 * rows + i : 3 * rows + i + 8, :],
        )
    below = acc[4 * rows : 4 * rows + 8, :]
    sub = lax.broadcasted_iota(I32, (8, cols), 0)
    stay = jnp.sum(jnp.where(sub < 2, below, 0.0), axis=0, keepdims=True)
    pushed = jnp.sum(jnp.where((sub >= 2) & (sub < 4), below, 0.0), axis=0, keepdims=True)
    first = lax.broadcasted_iota(I32, (8, cols), 0) == 0
    spilled = join(jnp.where(first, stay, 0.0), jnp.where(first, pushed, 0.0))
    grid[rows : rows + 8, :] = spilled

    @pl.when(lax.axis_index("rows") == lax.axis_size("rows") - 1)
    def _():
        tail = grid[rows - 8 : rows, :]
        sub8 = lax.broadcasted_iota(I32, (8, wide), 0)
        spill_row = jnp.broadcast_to(grid[rows : rows + 1, :], (8, wide))
        grid[rows - 8 : rows, :] = tail + jnp.where(sub8 == 7, spill_row, 0.0)
        grid[rows : rows + 8, :] = jnp.zeros((8, wide), F32)

    @pl.when(lax.axis_index("cols") == lax.axis_size("cols") - 1)
    def _():
        for i in range(0, rows + 8, 8):
            line = grid[i : i + 8, :]
            moved = jnp.where(lane == cols - 1, pltpu.roll(line, wide - 1, 1), 0.0)
            grid[i : i + 8, :] = jnp.where(lane < cols, line + moved, 0.0)


def gather_parts(cap, n_cols, kinds, pieces, ra_ref, rb_ref, groups):
    step = kinds * cap
    for dst, offset in groups:
        size = 2 * cap
        for k in range(n_cols):
            dst[k * size : (k + 1) * size, :] = pieces[k][offset : offset + size, :]
            for index, other in ((1, ra_ref), (2, rb_ref)):
                at = (index * n_cols + k) * size
                dst[at : at + size, :] = other[k * step + offset : k * step + offset + size, :]


def first_deposit_kernel(rows, cols, cap, n_cols, *refs):
    pieces = refs[:n_cols]
    ra_ref, rb_ref = refs[n_cols : n_cols + 2]
    grid, sa_ref, sb_ref, masses = refs[n_cols + 2 : n_cols + 6]
    moves, acc, lhs, rhs, slots = refs[n_cols + 6 :]
    chunks = 3 * n_cols
    gather_parts(
        cap, n_cols, 4, pieces, ra_ref, rb_ref, ((moves, 0), (masses, 2 * cap))
    )
    for ref in (moves, masses):
        ref[2 * cap * chunks :, :] = jnp.zeros((2 * cap, 128), F32)
    deposit_grid(rows, cols, cap, chunks, moves, masses, acc, lhs, rhs, slots, grid)
    row_even = lax.axis_index("rows") % 2 == 0
    south_going = grid[rows - 7 : rows + 1, :]
    north_going = grid[0:8, :]
    sa_ref[...] = pick(row_even, south_going, north_going)
    sb_ref[...] = pick(row_even, north_going, south_going)


def last_deposit_kernel(rows, cols, cap, n_cols, *refs):
    pieces = refs[:n_cols]
    ra_ref, rb_ref, masses = refs[n_cols : n_cols + 3]
    grid, row_ref, col_ref, corner_ref = refs[n_cols + 3 : n_cols + 7]
    moves, acc, lhs, rhs, slots = refs[n_cols + 7 :]
    chunks = 3 * n_cols
    gather_parts(cap, n_cols, 2, pieces, ra_ref, rb_ref, ((moves, 0),))
    moves[2 * cap * chunks :, :] = jnp.zeros((2 * cap, 128), F32)
    deposit_grid(rows, cols, cap, chunks, moves, masses, acc, lhs, rhs, slots, grid)
    row_ref[...] = grid[rows : rows + 8, 0:cols]
    corner_ref[...] = grid[rows : rows + 8, cols : cols + 128]
    col_ref[...] = flipped(grid[0:rows, cols : cols + 128])[0:8]


def edge_mid_kernel(rows, cols, g_ref, a_ref, b_ref, d_ref, ca_ref, cb_ref):
    row_even = lax.axis_index("rows") % 2 == 0
    col_even = lax.axis_index("cols") % 2 == 0
    wide = cols + 128
    north = pick(row_even, b_ref[...], a_ref[...])
    south = pick(row_even, a_ref[...], b_ref[...])
    d_ref[0:PAD, :] = jnp.zeros((PAD, wide), F32)
    d_ref[PAD : PAD + rows, :] = g_ref[0:rows, :]
    d_ref[PAD + rows : PAD + rows + 8, :] = south + g_ref[rows : rows + 8, :]
    d_ref[PAD + rows + 8 :, :] = jnp.zeros((d_ref.shape[0] - PAD - rows - 8, wide), F32)
    d_ref[PAD - 7 : PAD + 1, :] = d_ref[PAD - 7 : PAD + 1, :] + north
    west_going = flipped(d_ref[:, 0:128])[0:EDGE]
    east_going = flipped(d_ref[:, cols - 128 : cols])[128 - EDGE : 128]
    spilled = flipped(d_ref[:, cols : cols + 128])[0:EDGE]
    ca_ref[0:EDGE, :] = pick(col_even, east_going, west_going)
    cb_ref[0:EDGE, :] = pick(col_even, west_going, east_going)
    ca_ref[EDGE:, :] = pick(col_even, spilled, 0.0)
    cb_ref[EDGE:, :] = pick(col_even, 0.0, spilled)


def final_kernel(rows, cols, g_ref, m_ref, row_in, col_in, corner_in, total_ref, out_ref):
    n_rows, n_cols = lax.axis_size("rows"), lax.axis_size("cols")
    half_scale = 0.5 * ((rows * cols * n_rows * n_cols) / total_ref[0:1, 0:1])
    out_ref[...] = 0.5 * m_ref[...] + half_scale * g_ref[0:rows, 0:cols]
    out_ref[0:8, :] = out_ref[0:8, :] + half_scale * row_in[...]
    out_ref[0:8, 0:128] = out_ref[0:8, 0:128] + half_scale * corner_in[...]
    beside = jnp.concatenate([col_in[...], jnp.zeros((120, col_in.shape[1]), F32)], axis=0)
    out_ref[:, 0:128] = out_ref[:, 0:128] + half_scale * unflipped(beside, rows)


def exchange_columns(outs):
    n_cols = len(outs)
    return [outs[0]] + [xor_permute(outs[k], "cols", k) for k in range(1, n_cols)]


def exchange_rows(pieces, kinds, cap, extra=None):
    step = kinds * cap
    first = [piece[step : 2 * step] for piece in pieces]
    second = [piece[2 * step : 3 * step] for piece in pieces]
    if extra is not None:
        first.append(extra)
    return swap_both(jnp.concatenate(first), jnp.concatenate(second), "rows")


def body(terminal_value, density_start, start_cells, offsets, weights, dest_tiles, end_cells):
    rows, cols = terminal_value.shape
    n_rows, n_cols = lax.axis_size("rows"), lax.axis_size("cols")
    blocks = dest_tiles.shape[0]
    cap = blocks // 4
    chunks = 3 * n_cols
    wide, tall = cols + 128, rows + 2 * PAD
    flat = -(-tall // 128) * 128
    starts = start_cells.reshape(blocks, 128)
    wts = weights.reshape(blocks, 128)
    ends = end_cells.reshape(blocks, 128)
    row_even = lax.axis_index("rows") % 2 == 0

    south_going = jnp.concatenate([terminal_value[rows - EDGE :], density_start[rows - EDGE :]])
    north_going = jnp.concatenate([terminal_value[:EDGE], density_start[:EDGE]])
    ra, rb = swap_both(
        jnp.where(row_even, south_going, north_going),
        jnp.where(row_even, north_going, south_going),
        "rows",
    )
    ue, me, ca, cb = vmem_call(
        functools.partial(start_mid_kernel, rows, cols),
        (shape(tall, wide), shape(tall, wide), shape(2 * EDGE, flat), shape(2 * EDGE, flat)),
        4,
    )(terminal_value, density_start, ra, rb)
    ca, cb = swap_both(ca, cb, "cols")
    sweep_scratch = [
        pltpu.VMEM((tall, wide), F32),
        pltpu.VMEM((tall, wide), F32),
    ]

    def sample_scratch(part_rows):
        return [
            pltpu.VMEM((6 * rows, cols), BF16),
            pltpu.VMEM((n_cols * part_rows, 128), F32),
            pltpu.SMEM((blocks,), I32),
            pltpu.SMEM((chunks,), I32),
        ]

    deposit_scratch = [
        pltpu.VMEM((2 * cap * (chunks + 1), 128), F32),
        pltpu.VMEM((4 * rows + 16, cols), F32),
        pltpu.VMEM((4 * rows + 16, GROUP * 128), BF16),
        pltpu.VMEM((cols, GROUP * 128), BF16),
        pltpu.SMEM((chunks * cap + GROUP,), I32),
    ]
    part_rows = 12 * cap + EDGE
    *outs, ue, me = vmem_call(
        functools.partial(first_kernel, rows, cols, blocks, cap, n_cols),
        tuple([shape(part_rows, 128)] * n_cols + [shape(tall, wide)] * 2),
        9,
        sweep_scratch + sample_scratch(part_rows),
        smem_in=(8,),
    )(ue, me, ca, cb, starts, offsets, wts, ends, dest_tiles)
    pieces = exchange_columns(outs)
    total = sum(piece[part_rows - EDGE :] for piece in pieces)
    ra, rb = exchange_rows(pieces, 4, cap, total)
    total = total + ra[4 * n_cols * cap :]
    bit = 2
    while bit < n_rows:
        total = total + xor_permute(total, "rows", bit)
        bit *= 2
    grid, ea, eb, masses = vmem_call(
        functools.partial(first_deposit_kernel, rows, cols, cap, n_cols),
        (
            shape(rows + 8, wide),
            shape(8, wide),
            shape(8, wide),
            shape(2 * cap * (chunks + 1), 128),
        ),
        n_cols + 2,
        deposit_scratch,
    )(*pieces, ra, rb)
    ea, eb = swap_both(ea, eb, "rows")
    deposit, ca, cb = vmem_call(
        functools.partial(edge_mid_kernel, rows, cols),
        (shape(tall, wide), shape(2 * EDGE, flat), shape(2 * EDGE, flat)),
        3,
    )(grid, ea, eb)
    ca, cb = swap_both(ca, cb, "cols")
    part_rows = 6 * cap
    *outs, value, density = vmem_call(
        functools.partial(again_kernel, rows, cols, blocks, cap, n_cols),
        tuple([shape(part_rows, 128)] * n_cols + [shape(rows, cols)] * 2),
        9,
        sweep_scratch + [pltpu.VMEM((tall, wide), F32)] + sample_scratch(part_rows),
        smem_in=(8,),
    )(ue, me, deposit, ca, cb, total, starts, offsets, dest_tiles)
    pieces = exchange_columns(outs)
    ra, rb = exchange_rows(pieces, 2, cap)
    grid, below, beside, corner = vmem_call(
        functools.partial(last_deposit_kernel, rows, cols, cap, n_cols),
        (shape(rows + 8, wide), shape(8, cols), shape(8, rows), shape(8, 128)),
        n_cols + 3,
        deposit_scratch,
    )(*pieces, ra, rb, masses)
    below = lax.ppermute(below, "rows", [(i, i + 1) for i in range(n_rows - 1)])
    beside = lax.ppermute(beside, "cols", [(i, i + 1) for i in range(n_cols - 1)])
    corner = lax.ppermute(
        corner,
        ("rows", "cols"),
        [
            (r * n_cols + c, (r + 1) * n_cols + c + 1)
            for r in range(n_rows - 1)
            for c in range(n_cols - 1)
        ],
    )
    density = vmem_call(functools.partial(final_kernel, rows, cols), shape(rows, cols), 6)(
        grid, density, below, beside, corner, total
    )
    return (value, density)


def solution(mesh):
    in_specs = (
        P("rows", "cols"),
        P("rows", "cols"),
        P(("rows", "cols")),
        P(None, ("rows", "cols")),
        P(("rows", "cols")),
        P(("rows", "cols")),
        P(("rows", "cols")),
    )
    out_specs = (P("rows", "cols"), P("rows", "cols"))
    return jax.shard_map(body, mesh=mesh, in_specs=in_specs, out_specs=out_specs, check_vma=False)
```

time: 324 us -> 134 us (0.41)
  the two profiles are of different devices: /device:TPU:12 before, /device:TPU:11 now
where the time goes in v1:
time: 134 us; the launch traced here: 135 us
  Pallas kernels  56.5 us (42%)
  starting transfers between devices  38.2 us (29%)
  waiting for transfers between devices  28.7 us (21%)
  local copies, waits for them, and re-layouts  8.34 us (6%)
  other arithmetic  2.02 us (2%)
    ppermute x6, starting transfers between devices, swap_both(): lax.ppermute(second, axis, pairs_b)  18.3 us
    ppermute x6, waiting for transfers between devices, swap_both(): lax.ppermute(second, axis, pairs_b)  14.6 us
    pallas_call x1, Pallas kernels, body(): vmem_call(functools.partial(first_deposit_kernel, rows, cols, cap, n_cols...  13.5 us
    pallas_call x1, Pallas kernels, body(): vmem_call(functools.partial(last_deposit_kernel, rows, cols, cap, n_cols)...  13.5 us
    pallas_call x1, Pallas kernels, body(): vmem_call(functools.partial(first_kernel, rows, cols, blocks, cap, n_cols...  11.9 us
    pallas_call x1, Pallas kernels, body(): vmem_call(functools.partial(again_kernel, rows, cols, blocks, cap, n_cols...  11.9 us
    ppermute x8, waiting for transfers between devices, xor_permute(): lax.ppermute(value, axis, [(i, i ^ bit) for i in range(lax.axis_size(axis...  11 us
    unnamed x46, local copies, waits for them, and re-layouts  6.1 us
  transfers between devices with their start and end apart: 23, of which 12 were waited for; matrix products, arithmetic and copies ran while one was open for 2% of the time, Pallas kernels for 0%

profile of v1, /device:TPU:11, one launch (start us, length us, event | category | flops | bytes accessed | tf_op | source)
XLA Modules:
  0.0 134.7 jit_solution(15404940689525749809)
XLA Ops:
  0.6 0.8 fusion.2
  1.4 3.7 %collective-permute-start.1 = (f32[16,512]{1,0:T(8,128)S(1)}, f32[16,512]{1,0:T(8,128)S(1)}, u32[]{:S(2)}, u32[]{:S(2)}) collective-permute-start(f32[16,512]{1,0:T(8,128)S(1)} %get-tuple-element.62), channel_id=1, source_target_pairs={{4,8},{8,4},{12,16},{16,12},{20,24},{24,20},{5,9},{9,5},{13,17},{1... | collective-permute-start | bytes 98312 | tf_op jit(solution)/shard_map/ppermute | solution.py:26
  5.2 2.7 %collective-permute-done.1.b_ref = f32[16,512]{1,0:T(8,128)S(1)} collective-permute-done((f32[16,512]{1,0:T(8,128)S(1)}, f32[16,512]{1,0:T(8,128)S(1)}, u32[]{:S(2)}, u32[]{:S(2)}) %collective-permute-start.1) | collective-permute-done | bytes 32800 | tf_op jit(solution)/shard_map/ppermute | solution.py:26
  7.9 0.6 copy-done.10
  8.5 0.6 copy-done.11
  9.1 2.1 %shard_map.86 = (f32[160,640]{1,0:T(8,128)}, f32[160,640]{1,0:T(8,128)}, f32[16,256]{1,0:T(8,128)}, f32[16,256]{1,0:T(8,128)}) custom-call(f32[128,512]{1,0:T(8,128)} %u_ref.1, f32[128,512]{1,0:T(8,128)} %m_ref.1, f32[16,512]{1,0:T(8,128)} %copy-done.11, f32[16,512]{1,0:T(8,128)} %copy-done.10), custom_call_target="tpu_custom_call" | custom-call | tf_op jit(solution)/shard_map/pallas_call | solution.py:461
  11.3 4.3 %collective-permute-start.3 = (f32[16,256]{1,0:T(8,128)}, f32[16,256]{1,0:T(8,128)S(1)}, u32[]{:S(2)}, u32[]{:S(2)}) collective-permute-start(f32[16,256]{1,0:T(8,128)} %get-tuple-element.32), channel_id=1, source_target_pairs={{1,2},{2,1},{5,6},{6,5},{9,10},{10,9},{13,14},{14,13},{17,18},{18,... | collective-permute-start | bytes 49160 | tf_op jit(solution)/shard_map/ppermute | solution.py:26
  15.7 1.6 %collective-permute-done.3.refs_3_ = f32[16,256]{1,0:T(8,128)S(1)} collective-permute-done((f32[16,256]{1,0:T(8,128)}, f32[16,256]{1,0:T(8,128)S(1)}, u32[]{:S(2)}, u32[]{:S(2)}) %collective-permute-start.3) | collective-permute-done | bytes 16416 | tf_op jit(solution)/shard_map/ppermute | solution.py:26
  17.3 0.6 copy-done.18
  17.9 11.9 %shard_map.87 = (f32[104,128]{1,0:T(8,128)}, f32[104,128]{1,0:T(8,128)}, f32[104,128]{1,0:T(8,128)}, f32[104,128]{1,0:T(8,128)}, f32[160,640]{1,0:T(8,128)}, /*index=5*/f32[160,640]{1,0:T(8,128)}) custom-call(f32[160,640]{1,0:T(8,128)} %get-tuple-element.29.refs_0_, f32[160,640]{1,0:T(8,128)} %get-tuple-element.30.refs_1_, f32[16,256]{1,0:T(8,128)} %copy-done.17, ...), custom_call_target="tpu_custom_call" | custom-call | tf_op jit(solution)/shard_map/pallas_call | solution.py:488
  29.8 2.3 %collective-permute-start.5 = (f32[104,128]{1,0:T(8,128)}, f32[104,128]{1,0:T(8,128)S(1)}, u32[]{:S(2)}, u32[]{:S(2)}) collective-permute-start(f32[104,128]{1,0:T(8,128)} %get-tuple-element.37), channel_id=1, source_target_pairs={{0,2},{1,3},{2,0},{3,1},{4,6},{5,7},{6,4},{7,5},{8,10},{9,11},{10,... | collective-permute-start | bytes 159752 | tf_op jit(solution)/shard_map/ppermute | solution.py:30
  32.4 0.7 fusion.4
  33.2 1.3 collective-permute-done.5.refs_2_
  34.5 2.5 %collective-permute-done.6.refs_3_ = f32[104,128]{1,0:T(8,128)S(1)} collective-permute-done((f32[104,128]{1,0:T(8,128)}, f32[104,128]{1,0:T(8,128)S(1)}, u32[]{:S(2)}, u32[]{:S(2)}) %collective-permute-start.6) | collective-permute-done | bytes 53280 | tf_op jit(solution)/shard_map/ppermute | solution.py:30
  37.0 0.7 constant_dynamic-update-slice_fusion
  37.7 1.8 %collective-permute-start.7 = (f32[136,128]{1,0:T(8,128)S(1)}, f32[136,128]{1,0:T(8,128)S(1)}, u32[]{:S(2)}, u32[]{:S(2)}) collective-permute-start(f32[136,128]{1,0:T(8,128)S(1)} %get-tuple-element.56), channel_id=1, source_target_pairs={{0,4},{4,0},{8,12},{12,8},{16,20},{20,16},{24,28},{28,24},{1,5},{5... | collective-permute-start | bytes 208904 | tf_op jit(solution)/shard_map/ppermute | solution.py:26
  39.6 3.5 %collective-permute-start.8 = (f32[128,128]{1,0:T(8,128)S(1)}, f32[128,128]{1,0:T(8,128)S(1)}, u32[]{:S(2)}, u32[]{:S(2)}) collective-permute-start(f32[128,128]{1,0:T(8,128)S(1)} %pad_maximum_fusion), channel_id=1, source_target_pairs={{4,8},{8,4},{12,16},{16,12},{20,24},{24,20},{5,9},{9,5},{13,17},{1... | collective-permute-start | bytes 196616 | tf_op jit(solution)/shard_map/ppermute | solution.py:26
  43.1 2.9 %collective-permute-done.8.refs_5_ = f32[128,128]{1,0:T(8,128)S(1)} collective-permute-done((f32[128,128]{1,0:T(8,128)S(1)}, f32[128,128]{1,0:T(8,128)S(1)}, u32[]{:S(2)}, u32[]{:S(2)}) %collective-permute-start.8) | collective-permute-done | bytes 65568 | tf_op jit(solution)/shard_map/ppermute | solution.py:26
  46.1 0.6 copy-done.7
  46.7 0.6 copy-done.3
  47.3 13.5 %shard_map.88 = (f32[136,640]{1,0:T(8,128)}, f32[8,640]{1,0:T(8,128)}, f32[8,640]{1,0:T(8,128)}, f32[208,128]{1,0:T(8,128)}) custom-call(f32[104,128]{1,0:T(8,128)} %get-tuple-element.35.refs_0_, f32[104,128]{1,0:T(8,128)} %copy-done, f32[104,128]{1,0:T(8,128)} %copy-done.1, f32[104,128]{1,0:T(8,128)} %copy-done.2, f32[136,128]{1,0:T(8,128)} %copy-done.3, ...), custom_call_target="tpu_custom_call" | custom-call | tf_op jit(solution)/shard_map/pallas_call | solution.py:503
  60.8 1.9 %collective-permute-start.10 = (f32[8,640]{1,0:T(8,128)}, f32[8,640]{1,0:T(8,128)S(1)}, u32[]{:S(2)}, u32[]{:S(2)}) collective-permute-start(f32[8,640]{1,0:T(8,128)} %get-tuple-element.41), channel_id=1, source_target_pairs={{4,8},{8,4},{12,16},{16,12},{20,24},{24,20},{5,9},{9,5},{13,17},{1... | collective-permute-start | bytes 61448 | tf_op jit(solution)/shard_map/ppermute | solution.py:26
  62.8 4.3 %collective-permute-done.10.b_ref = f32[8,640]{1,0:T(8,128)S(1)} collective-permute-done((f32[8,640]{1,0:T(8,128)}, f32[8,640]{1,0:T(8,128)S(1)}, u32[]{:S(2)}, u32[]{:S(2)}) %collective-permute-start.10) | collective-permute-done | bytes 20512 | tf_op jit(solution)/shard_map/ppermute | solution.py:26
  67.0 0.6 copy-done.13
  67.6 1.9 %shard_map.89 = (f32[160,640]{1,0:T(8,128)}, f32[16,256]{1,0:T(8,128)}, f32[16,256]{1,0:T(8,128)}) custom-call(f32[136,640]{1,0:T(8,128)} %get-tuple-element.39.g_ref, f32[8,640]{1,0:T(8,128)} %copy-done.12, f32[8,640]{1,0:T(8,128)} %copy-done.13), custom_call_target="tpu_custom_call" | custom-call | tf_op jit(solution)/shard_map/pallas_call | solution.py:515
  69.5 1.9 %collective-permute-start.12 = (f32[16,256]{1,0:T(8,128)}, f32[16,256]{1,0:T(8,128)S(1)}, u32[]{:S(2)}, u32[]{:S(2)}) collective-permute-start(f32[16,256]{1,0:T(8,128)} %get-tuple-element.44), channel_id=1, source_target_pairs={{1,2},{2,1},{5,6},{6,5},{9,10},{10,9},{13,14},{14,13},{17,18},{18,... | collective-permute-start | bytes 49160 | tf_op jit(solution)/shard_map/ppermute | solution.py:26
  71.4 0.7 slice_add_fusion
  72.3 2.4 %collective-permute-done.13 = f32[8,128]{1,0:T(8,128)S(1)} collective-permute-done((f32[8,128]{1,0:T(8,128)S(1)}, f32[8,128]{1,0:T(8,128)S(1)}, u32[]{:S(2)}, u32[]{:S(2)}) %collective-permute-start.13) | collective-permute-done | bytes 4128 | tf_op jit(solution)/shard_map/ppermute | solution.py:30
  74.8 2.3 %collective-permute-done.14 = f32[8,128]{1,0:T(8,128)S(1)} collective-permute-done((f32[8,128]{1,0:T(8,128)S(1)}, f32[8,128]{1,0:T(8,128)S(1)}, u32[]{:S(2)}, u32[]{:S(2)}) %collective-permute-start.14) | collective-permute-done | bytes 4128 | tf_op jit(solution)/shard_map/ppermute | solution.py:30
  77.1 0.6 add.28.refs_5_.total_ref
  77.7 0.6 copy-done.14
  78.3 11.9 %shard_map.90 = (f32[48,128]{1,0:T(8,128)}, f32[48,128]{1,0:T(8,128)}, f32[48,128]{1,0:T(8,128)}, f32[48,128]{1,0:T(8,128)}, f32[128,512]{1,0:T(8,128)}, /*index=5*/f32[128,512]{1,0:T(8,128)}) custom-call(f32[160,640]{1,0:T(8,128)} %get-tuple-element.33.refs_0_, f32[160,640]{1,0:T(8,128)} %get-tuple-element.34.refs_1_, ...), custom_call_target="tpu_custom_call" | custom-call | tf_op jit(solution)/shard_map/pallas_call | solution.py:522
  90.4 0.7 fusion.8
  91.1 2.4 %collective-permute-start.16 = (f32[48,128]{1,0:T(8,128)}, f32[48,128]{1,0:T(8,128)S(1)}, u32[]{:S(2)}, u32[]{:S(2)}) collective-permute-start(f32[48,128]{1,0:T(8,128)} %get-tuple-element.48), channel_id=1, source_target_pairs={{0,2},{1,3},{2,0},{3,1},{4,6},{5,7},{6,4},{7,5},{8,10},{9,11},{10,... | collective-permute-start | bytes 73736 | tf_op jit(solution)/shard_map/ppermute | solution.py:30
  93.6 1.3 collective-permute-done.16.refs_2_
  95.0 1.2 collective-permute-done.17.refs_3_
  96.2 0.6 copy-done.6
  96.8 3.9 %collective-permute-start.18 = (f32[64,128]{1,0:T(8,128)S(1)}, f32[64,128]{1,0:T(8,128)S(1)}, u32[]{:S(2)}, u32[]{:S(2)}) collective-permute-start(f32[64,128]{1,0:T(8,128)S(1)} %pad_maximum_fusion.3), channel_id=1, source_target_pairs={{0,4},{4,0},{8,12},{12,8},{16,20},{20,16},{24,28},{28,24},{1,5},{5... | collective-permute-start | bytes 98312 | tf_op jit(solution)/shard_map/ppermute | solution.py:26
  100.7 3.0 %collective-permute-start.19 = (f32[64,128]{1,0:T(8,128)S(1)}, f32[64,128]{1,0:T(8,128)S(1)}, u32[]{:S(2)}, u32[]{:S(2)}) collective-permute-start(f32[64,128]{1,0:T(8,128)S(1)} %pad_maximum_fusion.4), channel_id=1, source_target_pairs={{4,8},{8,4},{12,16},{16,12},{20,24},{24,20},{5,9},{9,5},{13,17},{1... | collective-permute-start | bytes 98312 | tf_op jit(solution)/shard_map/ppermute | solution.py:26
  103.7 3.1 %collective-permute-done.19.refs_5_ = f32[64,128]{1,0:T(8,128)S(1)} collective-permute-done((f32[64,128]{1,0:T(8,128)S(1)}, f32[64,128]{1,0:T(8,128)S(1)}, u32[]{:S(2)}, u32[]{:S(2)}) %collective-permute-start.19) | collective-permute-done | bytes 32800 | tf_op jit(solution)/shard_map/ppermute | solution.py:26
  106.8 0.6 copy-done.9
  107.4 13.5 %shard_map.91 = (f32[136,640]{1,0:T(8,128)}, f32[8,512]{1,0:T(8,128)}, f32[8,128]{1,0:T(8,128)}, f32[8,128]{1,0:T(8,128)}) custom-call(f32[48,128]{1,0:T(8,128)} %get-tuple-element.46.refs_0_, f32[48,128]{1,0:T(8,128)} %copy-done.4, f32[48,128]{1,0:T(8,128)} %copy-done.5, f32[48,128]{1,0:T(8,128)} %copy-done.6, f32[64,128]{1,0:T(8,128)} %copy-done.8, ...), custom_call_target="tpu_custom_call" | custom-call | tf_op jit(solution)/shard_map/pallas_call | solution.py:531
  120.9 2.0 %collective-permute-start.20 = (f32[8,512]{1,0:T(8,128)}, f32[8,512]{1,0:T(8,128)S(1)}, u32[]{:S(2)}, u32[]{:S(2)}) collective-permute-start(f32[8,512]{1,0:T(8,128)} %get-tuple-element.53), channel_id=1, source_target_pairs={{0,4},{4,8},{8,12},{12,16},{16,20},{20,24},{24,28},{1,5},{5,9},{9,... | collective-permute-start | bytes 49160 | tf_op jit(solution)/shard_map/ppermute | solution.py:537
  123.0 4.2 %collective-permute-start.21 = (f32[8,128]{1,0:T(8,128)}, f32[8,128]{1,0:T(8,128)S(1)}, u32[]{:S(2)}, u32[]{:S(2)}) collective-permute-start(f32[8,128]{1,0:T(8,128)} %get-tuple-element.54), channel_id=1, source_target_pairs={{0,1},{1,2},{2,3},{4,5},{5,6},{6,7},{8,9},{9,10},{10,11},{12,13},{... | collective-permute-start | bytes 12296 | tf_op jit(solution)/shard_map/ppermute | solution.py:538
  127.2 1.9 %collective-permute-start.22 = (f32[8,128]{1,0:T(8,128)S(1)}, f32[8,128]{1,0:T(8,128)S(1)}, u32[]{:S(2)}, u32[]{:S(2)}) collective-permute-start(f32[8,128]{1,0:T(8,128)S(1)} %copy-done.22), channel_id=1, source_target_pairs={{0,5},{1,6},{2,7},{4,9},{5,10},{6,11},{8,13},{9,14},{10,15},{12,17... | collective-permute-start | bytes 12296 | tf_op jit(solution)/shard_map/ppermute | solution.py:539
  129.2 3.0 %collective-permute-done.22.corner_in = f32[8,128]{1,0:T(8,128)S(1)} collective-permute-done((f32[8,128]{1,0:T(8,128)S(1)}, f32[8,128]{1,0:T(8,128)S(1)}, u32[]{:S(2)}, u32[]{:S(2)}) %collective-permute-start.22) | collective-permute-done | bytes 4128 | tf_op jit(solution)/shard_map/ppermute | solution.py:539
  132.2 0.6 copy-done.20
  132.8 1.9 %shard_map.92 = f32[128,512]{1,0:T(8,128)} custom-call(f32[136,640]{1,0:T(8,128)} %get-tuple-element.51.g_ref, f32[128,512]{1,0:T(8,128)} %get-tuple-element.52.m_ref, f32[8,512]{1,0:T(8,128)} %copy-done.16, f32[8,128]{1,0:T(8,128)} %copy-done.19, f32[8,128]{1,0:T(8,128)} %copy-done.20, f32[8,128]{1,0:T(8,128)} %add.28.refs_5_.total_ref), custom_call_target="tpu_custom_call" | custom-call | tf_op jit(solution)/shard_map/pallas_call | solution.py:548
  (68 shorter events, 1.4 us)
Async XLA Ops:
  1.4 6.4 %collective-permute-start.1 = (f32[16,512]{1,0:T(8,128)S(1)}, f32[16,512]{1,0:T(8,128)S(1)}, u32[]{:S(2)}, u32[]{:S(2)}) collective-permute-start(f32[16,512]{1,0:T(8,128)S(1)} %get-tuple-element.62), channel_id=1, source_target_pairs={{4,8},{8,4},{12,16},{16,12},{20,24},{24,20},{5,9},{9,5},{13,17},{1... | collective-permute-start | bytes 98312 | tf_op jit(solution)/shard_map/ppermute | solution.py:26
  5.1 2.8 %collective-permute-start = (f32[16,512]{1,0:T(8,128)S(1)}, f32[16,512]{1,0:T(8,128)S(1)}, u32[]{:S(2)}, u32[]{:S(2)}) collective-permute-start(f32[16,512]{1,0:T(8,128)S(1)} %get-tuple-element.63), channel_id=1, source_target_pairs={{0,4},{4,0},{8,12},{12,8},{16,20},{20,16},{24,28},{28,24},{1,5},{5... | collective-permute-start | bytes 98312 | tf_op jit(solution)/shard_map/ppermute | solution.py:26
  7.9 0.6 copy-start.10
  8.5 0.6 copy-start.11
  11.2 4.5 %collective-permute-start.2 = (f32[16,256]{1,0:T(8,128)}, f32[16,256]{1,0:T(8,128)S(1)}, u32[]{:S(2)}, u32[]{:S(2)}) collective-permute-start(f32[16,256]{1,0:T(8,128)} %get-tuple-element.31), channel_id=1, source_target_pairs={{0,1},{1,0},{2,3},{3,2},{4,5},{5,4},{6,7},{7,6},{8,9},{9,8},{10,11... | collective-permute-start | bytes 49160 | tf_op jit(solution)/shard_map/ppermute | solution.py:26
  11.3 6.0 %collective-permute-start.3 = (f32[16,256]{1,0:T(8,128)}, f32[16,256]{1,0:T(8,128)S(1)}, u32[]{:S(2)}, u32[]{:S(2)}) collective-permute-start(f32[16,256]{1,0:T(8,128)} %get-tuple-element.32), channel_id=1, source_target_pairs={{1,2},{2,1},{5,6},{6,5},{9,10},{10,9},{13,14},{14,13},{17,18},{18,... | collective-permute-start | bytes 49160 | tf_op jit(solution)/shard_map/ppermute | solution.py:26
  15.7 1.6 %copy-start.17 = (f32[16,256]{1,0:T(8,128)}, f32[16,256]{1,0:T(8,128)S(1)}, u32[]{:S(2)}) copy-start(f32[16,256]{1,0:T(8,128)S(1)} %collective-permute-done.2.refs_2_) | copy-start | bytes 49156
  17.3 0.6 copy-start.18
  29.8 3.4 %collective-permute-start.4 = (f32[104,128]{1,0:T(8,128)}, f32[104,128]{1,0:T(8,128)S(1)}, u32[]{:S(2)}, u32[]{:S(2)}) collective-permute-start(f32[104,128]{1,0:T(8,128)} %get-tuple-element.36), channel_id=1, source_target_pairs={{0,1},{1,0},{2,3},{3,2},{4,5},{5,4},{6,7},{7,6},{8,9},{9,8},{10,11... | collective-permute-start | bytes 159752 | tf_op jit(solution)/shard_map/ppermute | solution.py:30
  29.8 4.7 %collective-permute-start.5 = (f32[104,128]{1,0:T(8,128)}, f32[104,128]{1,0:T(8,128)S(1)}, u32[]{:S(2)}, u32[]{:S(2)}) collective-permute-start(f32[104,128]{1,0:T(8,128)} %get-tuple-element.37), channel_id=1, source_target_pairs={{0,2},{1,3},{2,0},{3,1},{4,6},{5,7},{6,4},{7,5},{8,10},{9,11},{10,... | collective-permute-start | bytes 159752 | tf_op jit(solution)/shard_map/ppermute | solution.py:30
  32.1 4.9 %collective-permute-start.6 = (f32[104,128]{1,0:T(8,128)}, f32[104,128]{1,0:T(8,128)S(1)}, u32[]{:S(2)}, u32[]{:S(2)}) collective-permute-start(f32[104,128]{1,0:T(8,128)} %get-tuple-element.38), channel_id=1, source_target_pairs={{0,3},{1,2},{2,1},{3,0},{4,7},{5,6},{6,5},{7,4},{8,11},{9,10},{10,... | collective-permute-start | bytes 159752 | tf_op jit(solution)/shard_map/ppermute | solution.py:30
  33.2 3.8 %copy-start = (f32[104,128]{1,0:T(8,128)}, f32[104,128]{1,0:T(8,128)S(1)}, u32[]{:S(2)}) copy-start(f32[104,128]{1,0:T(8,128)S(1)} %collective-permute-done.4.refs_1_) | copy-start | bytes 159748
  34.5 2.5 %copy-start.1 = (f32[104,128]{1,0:T(8,128)}, f32[104,128]{1,0:T(8,128)S(1)}, u32[]{:S(2)}) copy-start(f32[104,128]{1,0:T(8,128)S(1)} %collective-permute-done.5.refs_2_) | copy-start | bytes 159748
  37.0 2.6 %copy-start.2 = (f32[104,128]{1,0:T(8,128)}, f32[104,128]{1,0:T(8,128)S(1)}, u32[]{:S(2)}) copy-start(f32[104,128]{1,0:T(8,128)S(1)} %collective-permute-done.6.refs_3_) | copy-start | bytes 159748
  37.7 8.3 %collective-permute-start.7 = (f32[136,128]{1,0:T(8,128)S(1)}, f32[136,128]{1,0:T(8,128)S(1)}, u32[]{:S(2)}, u32[]{:S(2)}) collective-permute-start(f32[136,128]{1,0:T(8,128)S(1)} %get-tuple-element.56), channel_id=1, source_target_pairs={{0,4},{4,0},{8,12},{12,8},{16,20},{20,16},{24,28},{28,24},{1,5},{5... | collective-permute-start | bytes 208904 | tf_op jit(solution)/shard_map/ppermute | solution.py:26
  39.6 6.5 %collective-permute-start.8 = (f32[128,128]{1,0:T(8,128)S(1)}, f32[128,128]{1,0:T(8,128)S(1)}, u32[]{:S(2)}, u32[]{:S(2)}) collective-permute-start(f32[128,128]{1,0:T(8,128)S(1)} %pad_maximum_fusion), channel_id=1, source_target_pairs={{4,8},{8,4},{12,16},{16,12},{20,24},{24,20},{5,9},{9,5},{13,17},{1... | collective-permute-start | bytes 196616 | tf_op jit(solution)/shard_map/ppermute | solution.py:26
  46.1 0.6 copy-start.7
  46.7 0.6 copy-start.3
  60.8 1.9 %collective-permute-start.9 = (f32[8,640]{1,0:T(8,128)}, f32[8,640]{1,0:T(8,128)S(1)}, u32[]{:S(2)}, u32[]{:S(2)}) collective-permute-start(f32[8,640]{1,0:T(8,128)} %get-tuple-element.40), channel_id=1, source_target_pairs={{0,4},{4,0},{8,12},{12,8},{16,20},{20,16},{24,28},{28,24},{1,5},{5... | collective-permute-start | bytes 61448 | tf_op jit(solution)/shard_map/ppermute | solution.py:26
  60.8 6.2 %collective-permute-start.10 = (f32[8,640]{1,0:T(8,128)}, f32[8,640]{1,0:T(8,128)S(1)}, u32[]{:S(2)}, u32[]{:S(2)}) collective-permute-start(f32[8,640]{1,0:T(8,128)} %get-tuple-element.41), channel_id=1, source_target_pairs={{4,8},{8,4},{12,16},{16,12},{20,24},{24,20},{5,9},{9,5},{13,17},{1... | collective-permute-start | bytes 61448 | tf_op jit(solution)/shard_map/ppermute | solution.py:26
  62.8 4.3 %copy-start.12 = (f32[8,640]{1,0:T(8,128)}, f32[8,640]{1,0:T(8,128)S(1)}, u32[]{:S(2)}) copy-start(f32[8,640]{1,0:T(8,128)S(1)} %collective-permute-done.9.a_ref) | copy-start | bytes 61444
  67.0 0.6 copy-start.13
  69.5 8.2 %collective-permute-start.11 = (f32[16,256]{1,0:T(8,128)}, f32[16,256]{1,0:T(8,128)S(1)}, u32[]{:S(2)}, u32[]{:S(2)}) collective-permute-start(f32[16,256]{1,0:T(8,128)} %get-tuple-element.43), channel_id=1, source_target_pairs={{0,1},{1,0},{2,3},{3,2},{4,5},{5,4},{6,7},{7,6},{8,9},{9,8},{10,11... | collective-permute-start | bytes 49160 | tf_op jit(solution)/shard_map/ppermute | solution.py:26
  69.5 8.2 %collective-permute-start.12 = (f32[16,256]{1,0:T(8,128)}, f32[16,256]{1,0:T(8,128)S(1)}, u32[]{:S(2)}, u32[]{:S(2)}) collective-permute-start(f32[16,256]{1,0:T(8,128)} %get-tuple-element.44), channel_id=1, source_target_pairs={{1,2},{2,1},{5,6},{6,5},{9,10},{10,9},{13,14},{14,13},{17,18},{18,... | collective-permute-start | bytes 49160 | tf_op jit(solution)/shard_map/ppermute | solution.py:26
  72.1 2.5 %collective-permute-start.13 = (f32[8,128]{1,0:T(8,128)S(1)}, f32[8,128]{1,0:T(8,128)S(1)}, u32[]{:S(2)}, u32[]{:S(2)}) collective-permute-start(f32[8,128]{1,0:T(8,128)S(1)} %slice_add_fusion), channel_id=1, source_target_pairs={{0,8},{4,12},{8,0},{12,4},{16,24},{20,28},{24,16},{28,20},{1,9},{5... | collective-permute-start | bytes 12296 | tf_op jit(solution)/shard_map/ppermute | solution.py:30
  74.7 2.5 %collective-permute-start.14 = (f32[8,128]{1,0:T(8,128)S(1)}, f32[8,128]{1,0:T(8,128)S(1)}, u32[]{:S(2)}, u32[]{:S(2)}) collective-permute-start(f32[8,128]{1,0:T(8,128)S(1)} %add.27), channel_id=1, source_target_pairs={{0,16},{4,20},{8,24},{12,28},{16,0},{20,4},{24,8},{28,12},{1,17},{... | collective-permute-start | bytes 12296 | tf_op jit(solution)/shard_map/ppermute | solution.py:30
  77.7 0.6 copy-start.14
  77.7 0.6 copy-start.15
  90.2 3.3 %copy-start.21 = (f32[48,128]{1,0:T(8,128)S(1)}, f32[48,128]{1,0:T(8,128)}, u32[]{:S(2)}) copy-start(f32[48,128]{1,0:T(8,128)} %get-tuple-element.49) | copy-start | bytes 73732
  90.2 3.4 %collective-permute-start.15 = (f32[48,128]{1,0:T(8,128)}, f32[48,128]{1,0:T(8,128)S(1)}, u32[]{:S(2)}, u32[]{:S(2)}) collective-permute-start(f32[48,128]{1,0:T(8,128)} %get-tuple-element.47), channel_id=1, source_target_pairs={{0,1},{1,0},{2,3},{3,2},{4,5},{5,4},{6,7},{7,6},{8,9},{9,8},{10,11... | collective-permute-start | bytes 73736 | tf_op jit(solution)/shard_map/ppermute | solution.py:30
  91.1 3.9 %collective-permute-start.16 = (f32[48,128]{1,0:T(8,128)}, f32[48,128]{1,0:T(8,128)S(1)}, u32[]{:S(2)}, u32[]{:S(2)}) collective-permute-start(f32[48,128]{1,0:T(8,128)} %get-tuple-element.48), channel_id=1, source_target_pairs={{0,2},{1,3},{2,0},{3,1},{4,6},{5,7},{6,4},{7,5},{8,10},{9,11},{10,... | collective-permute-start | bytes 73736 | tf_op jit(solution)/shard_map/ppermute | solution.py:30
  93.5 2.7 %collective-permute-start.17 = (f32[48,128]{1,0:T(8,128)S(1)}, f32[48,128]{1,0:T(8,128)S(1)}, u32[]{:S(2)}, u32[]{:S(2)}) collective-permute-start(f32[48,128]{1,0:T(8,128)S(1)} %copy-done.21), channel_id=1, source_target_pairs={{0,3},{1,2},{2,1},{3,0},{4,7},{5,6},{6,5},{7,4},{8,11},{9,10},{10,... | collective-permute-start | bytes 73736 | tf_op jit(solution)/shard_map/ppermute | solution.py:30
  93.6 1.3 copy-start.4
  95.0 1.2 copy-start.5
  96.2 0.6 copy-start.6
  96.8 6.9 %collective-permute-start.18 = (f32[64,128]{1,0:T(8,128)S(1)}, f32[64,128]{1,0:T(8,128)S(1)}, u32[]{:S(2)}, u32[]{:S(2)}) collective-permute-start(f32[64,128]{1,0:T(8,128)S(1)} %pad_maximum_fusion.3), channel_id=1, source_target_pairs={{0,4},{4,0},{8,12},{12,8},{16,20},{20,16},{24,28},{28,24},{1,5},{5... | collective-permute-start | bytes 98312 | tf_op jit(solution)/shard_map/ppermute | solution.py:26
  100.7 6.1 %collective-permute-start.19 = (f32[64,128]{1,0:T(8,128)S(1)}, f32[64,128]{1,0:T(8,128)S(1)}, u32[]{:S(2)}, u32[]{:S(2)}) collective-permute-start(f32[64,128]{1,0:T(8,128)S(1)} %pad_maximum_fusion.4), channel_id=1, source_target_pairs={{4,8},{8,4},{12,16},{16,12},{20,24},{24,20},{5,9},{9,5},{13,17},{1... | collective-permute-start | bytes 98312 | tf_op jit(solution)/shard_map/ppermute | solution.py:26
  103.7 3.1 %copy-start.8 = (f32[64,128]{1,0:T(8,128)}, f32[64,128]{1,0:T(8,128)S(1)}, u32[]{:S(2)}) copy-start(f32[64,128]{1,0:T(8,128)S(1)} %collective-permute-done.18.refs_4_) | copy-start | bytes 98308
  106.8 0.6 copy-start.9
  120.9 6.3 %copy-start.22 = (f32[8,128]{1,0:T(8,128)S(1)}, f32[8,128]{1,0:T(8,128)}, u32[]{:S(2)}) copy-start(f32[8,128]{1,0:T(8,128)} %get-tuple-element.55) | copy-start | bytes 12292
  120.9 11.2 %collective-permute-start.20 = (f32[8,512]{1,0:T(8,128)}, f32[8,512]{1,0:T(8,128)S(1)}, u32[]{:S(2)}, u32[]{:S(2)}) collective-permute-start(f32[8,512]{1,0:T(8,128)} %get-tuple-element.53), channel_id=1, source_target_pairs={{0,4},{4,8},{8,12},{12,16},{16,20},{20,24},{24,28},{1,5},{5,9},{9,... | collective-permute-start | bytes 49160 | tf_op jit(solution)/shard_map/ppermute | solution.py:537
  123.0 6.2 %collective-permute-start.21 = (f32[8,128]{1,0:T(8,128)}, f32[8,128]{1,0:T(8,128)S(1)}, u32[]{:S(2)}, u32[]{:S(2)}) collective-permute-start(f32[8,128]{1,0:T(8,128)} %get-tuple-element.54), channel_id=1, source_target_pairs={{0,1},{1,2},{2,3},{4,5},{5,6},{6,7},{8,9},{9,10},{10,11},{12,13},{... | collective-permute-start | bytes 12296 | tf_op jit(solution)/shard_map/ppermute | solution.py:538
  127.2 4.9 %collective-permute-start.22 = (f32[8,128]{1,0:T(8,128)S(1)}, f32[8,128]{1,0:T(8,128)S(1)}, u32[]{:S(2)}, u32[]{:S(2)}) collective-permute-start(f32[8,128]{1,0:T(8,128)S(1)} %copy-done.22), channel_id=1, source_target_pairs={{0,5},{1,6},{2,7},{4,9},{5,10},{6,11},{8,13},{9,14},{10,15},{12,17... | collective-permute-start | bytes 12296 | tf_op jit(solution)/shard_map/ppermute | solution.py:539
  129.2 3.0 %copy-start.19 = (f32[8,128]{1,0:T(8,128)}, f32[8,128]{1,0:T(8,128)S(1)}, u32[]{:S(2)}) copy-start(f32[8,128]{1,0:T(8,128)S(1)} %collective-permute-done.21.col_in) | copy-start | bytes 12292
  132.2 0.6 copy-start.20
  132.2 0.6 copy-start.16
